TPU v7x, 256 devices: a whole 4x4x8 slice. The times are simulated.
256 devices in a mesh: lat: 8 (over x_hi, y), lon: 32 (over x_lo, z, core).
Axes of the slice: x: 4 (x_hi: 2, x_lo: 2; x = x_hi * 2 + x_lo), y: 4, z: 8, core: 2. Of those that a mesh axis runs over, the one named last changes fastest.
Arguments:
- tracer: float32 [100, 64, 4096], P(None, 'lat', 'lon'), may hold values from -100 to 100
- cotangent: float32 [100, 64, 4096], P(None, 'lat', 'lon'), may hold values from -6 to 6
- land_mask: int32 [64, 4096], P('lat', 'lon'), may hold values 0 or 1
- bottom: int32 [64, 4096], P('lat', 'lon'), may hold values from 25 to 100
- kappa: float32 [100], replicated, may hold values from 0.05 to 8
- w_in: bfloat16 [100, 512], replicated, may hold values from -0.625 to 0.625
- b_in: float32 [512], replicated, may hold values from -4 to 4
- w_out: bfloat16 [512, 100], replicated, may hold values from -0.25 to 0.25
- b_out: float32 [100], replicated, may hold values from 6 to 24
Outputs:
- tracer_adjoint: float32 [100, 64, 4096], P(None, 'lat', 'lon')
- grad_w_in: float32 [100, 512], replicated
- grad_b_in: float32 [512], replicated
- grad_w_out: float32 [512, 100], replicated
- grad_b_out: float32 [100], replicated
All inputs are finite; a program needn't handle non-finite values. No bound on the sum of `land_mask` on one device may be relied on, other than what follows from the above.
Results may differ from a plain program's by a relative error of at most 0.0069.
Values sent between devices are 32-bit elements; how exact they have to be, the bound alone decides.
A program may use at most 64 MiB of HBM per device.

v0:
```python
import math

import jax
import jax.numpy as jnp
from jax import lax
from jax.sharding import PartitionSpec as P

spread_coef = 0.15
level_eps = 1e-05


def with_halo(block, sides, width):
    for axis, dim in sides:
        count = lax.axis_size(axis)
        forward = [(i, i + 1) for i in range(count - 1)]
        forward.append((count - 1, 0))
        backward = [(target, source) for source, target in forward]
        low = lax.ppermute(
            lax.slice_in_dim(block, block.shape[dim] - width, None, axis=dim), axis, forward
        )
        high = lax.ppermute(lax.slice_in_dim(block, 0, width, axis=dim), axis, backward)
        block = jnp.concatenate([low, block, high], axis=dim)
    return block


def spread_local(field_pad, wet_pad):
    center = field_pad[:, 1:-1, 1:-1]
    wet_cells = wet_pad[:, 1:-1, 1:-1]
    neighbours = (
        (field_pad[:, 2:, 1:-1], wet_pad[:, 2:, 1:-1]),
        (field_pad[:, :-2, 1:-1], wet_pad[:, :-2, 1:-1]),
        (field_pad[:, 1:-1, :-2], wet_pad[:, 1:-1, :-2]),
        (field_pad[:, 1:-1, 2:], wet_pad[:, 1:-1, 2:]),
    )
    flux_total = jnp.zeros_like(center)
    for near_field, near_wet in neighbours:
        flux_total = flux_total + wet_cells * near_wet * (near_field - center)
    return center + spread_coef * flux_total


def column_solve(below, diagonal, above, right_side):

    def sweep_down(state_pair, row_items):
        ratio_prev, value_prev = state_pair
        below_row, diag_row, above_row, right_row = row_items
        pivot = diag_row - below_row * ratio_prev
        ratio_next = above_row / pivot
        value_next = (right_row - below_row * value_prev) / pivot
        return ((ratio_next, value_next), (ratio_next, value_next))

    zeros_row = jnp.zeros_like(right_side[0])
    _, (ratios, values) = lax.scan(
        sweep_down, (zeros_row, zeros_row), (below, diagonal, above, right_side), unroll=True
    )

    def sweep_up(later, row_items):
        ratio_row, value_row = row_items
        result_row = value_row - ratio_row * later
        return (result_row, result_row)

    _, solved = lax.scan(sweep_up, zeros_row, (ratios, values), reverse=True, unroll=True)
    return solved


def network(wet_tracer, radius, w_in, b_in, w_out, b_out):
    inputs = (wet_tracer / radius[:, None]).astype(jnp.bfloat16)
    pre_act = (
        lax.dot_general(w_in, inputs, (((0,), (0,)), ((), ())), preferred_element_type=jnp.float32)
        + b_in[:, None]
    )
    hidden = jax.nn.silu(pre_act).astype(jnp.bfloat16)
    logits = (
        lax.dot_general(w_out, hidden, (((0,), (0,)), ((), ())), preferred_element_type=jnp.float32)
        + b_out[:, None]
    )
    sinking = jax.nn.softplus(logits)
    return (inputs, pre_act, hidden, logits, sinking)


def coefficients(wet_cells, kappa_col, sinking):
    open_face = wet_cells * jnp.concatenate([wet_cells[1:], jnp.zeros_like(wet_cells[:1])], 0)
    down_coef = open_face * (kappa_col + sinking)
    up_coef = open_face * kappa_col
    prev_down = jnp.concatenate([jnp.zeros_like(down_coef[:1]), down_coef[:-1]], 0)
    prev_up = jnp.concatenate([jnp.zeros_like(up_coef[:1]), up_coef[:-1]], 0)
    diagonal = 1.0 + down_coef + prev_up
    return (open_face, down_coef, up_coef, prev_down, prev_up, diagonal)


def shards(tracer, cotangent, land_mask, bottom, kappa, w_in, b_in, w_out, b_out):
    level_count, lat_rows, lon_cols = tracer.shape
    column_count = lat_rows * lax.axis_size("lat") * lon_cols * lax.axis_size("lon")
    column_depth = (land_mask * bottom).astype(jnp.float32)
    stacked = jnp.concatenate([tracer, column_depth[None]], 0)
    padded = with_halo(stacked, (("lat", 1), ("lon", 2)), 1)
    lat_place = lax.axis_index("lat")
    upper_edge = jnp.where(lat_place == 0, 0.0, 1.0).astype(jnp.float32)
    lower_edge = jnp.where(lat_place == lax.axis_size("lat") - 1, 0.0, 1.0).astype(jnp.float32)
    lat_edge = jnp.concatenate(
        [upper_edge[None], jnp.ones((lat_rows,), jnp.float32), lower_edge[None]]
    )
    depth_pad = padded[-1] * lat_edge[:, None]
    level_ids = jnp.arange(level_count, dtype=jnp.float32)[:, None, None]
    wet_pad = (level_ids < depth_pad[None]).astype(jnp.float32)
    wet_cells = wet_pad[:, 1:-1, 1:-1]
    tracer_pad = padded[:level_count]
    mixed = spread_local(tracer_pad, wet_pad)
    wet_tracer = (wet_cells * tracer).reshape(level_count, -1)
    energy = lax.psum(jnp.sum(wet_tracer * wet_tracer, axis=1), ("lat", "lon"))
    radius = jnp.sqrt(energy / column_count + level_eps)
    inputs, pre_act, hidden, logits, sinking_flat = network(
        wet_tracer, radius, w_in, b_in, w_out, b_out
    )
    sinking = sinking_flat.reshape(tracer.shape)
    kappa_col = kappa[:, None, None]
    open_face, down_coef, up_coef, prev_down, prev_up, diagonal = coefficients(
        wet_cells, kappa_col, sinking
    )
    new_tracer = column_solve(-prev_down, diagonal, -up_coef, mixed)
    adjoint = column_solve(-prev_up, diagonal, -down_coef, cotangent)
    adjoint_pad = with_halo(adjoint, (("lat", 1), ("lon", 2)), 1)
    spread_back = spread_local(adjoint_pad, wet_pad)
    adjoint_next = jnp.concatenate([adjoint[1:], jnp.zeros_like(adjoint[:1])], 0)
    d_sinking = open_face * new_tracer * (adjoint_next - adjoint)
    d_logits = (d_sinking.reshape(level_count, -1) * jax.nn.sigmoid(logits)).astype(jnp.bfloat16)
    grad_out_t = lax.dot_general(
        d_logits, hidden, (((1,), (1,)), ((), ())), preferred_element_type=jnp.float32
    )
    grad_bout = jnp.sum(d_logits.astype(jnp.float32), axis=1)
    d_hidden = jnp.dot(w_out, d_logits, preferred_element_type=jnp.float32)
    gate_sig = jax.nn.sigmoid(pre_act)
    d_pre = (d_hidden * gate_sig * (1.0 + pre_act * (1.0 - gate_sig))).astype(jnp.bfloat16)
    grad_in = lax.dot_general(
        inputs, d_pre, (((1,), (1,)), ((), ())), preferred_element_type=jnp.float32
    )
    grad_bin = jnp.sum(d_pre.astype(jnp.float32), axis=1)[None]
    d_inputs = jnp.dot(w_in, d_pre, preferred_element_type=jnp.float32)
    level_part = jnp.sum(d_inputs * wet_tracer, axis=1)
    sum_in, sum_out_t, sum_bin, sum_bout, level_sum = lax.psum(
        (grad_in, grad_out_t, grad_bin, grad_bout, level_part), ("lat", "lon")
    )
    column_scale = 1.0 / math.sqrt(column_count)
    d_wet = (
        d_inputs / radius[:, None] - wet_tracer * (level_sum / (column_count * radius**3))[:, None]
    )
    tracer_adjoint = spread_back + wet_cells * d_wet.reshape(tracer.shape)
    grad_w_in = sum_in * column_scale
    grad_b_in = sum_bin[0] * column_scale
    grad_w_out = sum_out_t.T * column_scale
    grad_b_out = sum_bout * column_scale
    return (tracer_adjoint, grad_w_in, grad_b_in, grad_w_out, grad_b_out)


def solution(mesh):
    placed = (
        P(None, "lat", "lon"),
        P(None, "lat", "lon"),
        P("lat", "lon"),
        P("lat", "lon"),
        P(),
        P(),
        P(),
        P(),
        P(),
    )
    return jax.shard_map(
        shards,
        mesh=mesh,
        in_specs=placed,
        out_specs=(P(None, "lat", "lon"), P(), P(), P(), P()),
        check_vma=False,
    )
```

profile of v0, /device:TPU:1, one launch (start us, length us, event | category | flops | bytes accessed | tf_op | source)
XLA Modules:
  0.0 479.2 jit_solution(435788746220451003)
XLA Ops:
  7.9 1.2 pad_maximum_fusion.23
  9.1 2.2 collective-permute-start
  11.3 4.0 collective-permute-start.1
  15.3 1.4 collective-permute-done
  16.7 1.2 pad_maximum_fusion
  18.6 3.3 collective-permute-start.2
  23.2 2.2 collective-permute-done.3
  25.8 0.9 copy-done.2
  27.2 0.7 copy-done.4
  27.9 2.3 fusion.735
  30.3 0.8 copy.1030
  31.1 82.0 %psum.42 = f32[100]{0:T(128)S(1)} all-reduce(f32[100]{0:T(128)S(1)} %get-tuple-element.618), channel_id=1, replica_groups=mesh['lat'=8,'lon'=32] {'lat','lon'}, use_global_device_ids=true, to_apply=%region_1.2 | all-reduce | flops 100 | bytes 800 | tf_op jit(solution)/shard_map/psum | solution.py:109
  113.2 1.9 fusion.5
  117.7 1.1 fusion.15
  126.4 1.0 fusion.834
  127.4 1.0 convert_reduce_fusion
  128.4 1.0 copy-done.10
  129.4 1.0 fusion.543
  130.5 2.5 multiply_reduce_fusion
  133.0 2.2 collective-permute-start.4
  135.2 76.5 %all-reduce.4 = (f32[100]{0:T(128)S(1)}, f32[1,512]{1,0:T(1,128)S(1)}, f32[100]{0:T(128)S(1)}) all-reduce(f32[100]{0:T(128)S(1)} %get-tuple-element.826, f32[1,512]{1,0:T(1,128)S(1)} %bitcast.5569, f32[100]{0:T(128)S(1)} %get-tuple-element.15), channel_id=1, replica_groups=mesh['lat'=8,'lon'=32] {'lat','lon'}, use_global_device_ids=true, to_apply=%region_3.4 | all-reduce | flops 712 | bytes 5696 | tf_op jit(solution)/shard_map/psum | solution.py:139
  211.7 1.1 multiply_subtract_fusion
  213.6 1.2 fusion.832
  214.8 1.5 copy.1024
  216.2 2.4 collective-permute-start.6
  219.6 0.9 copy.1033
  220.9 1.2 collective-permute-done.7
  222.1 1.3 copy.1027
  223.4 3.0 fusion.9
  226.4 242.8 %all-reduce.8.cloned.1.call-done = (f32[100,512]{1,0:T(8,128)}, f32[100,512]{1,0:T(8,128)}) async-done(((f32[100,512]{1,0:T(8,128)}, f32[100,512]{1,0:T(8,128)}), (f32[100,512]{1,0:T(8,128)}, f32[100,512]{1,0:T(8,128)})) %all-reduce.8.cloned.1.call-update) | async-done | bytes 409616 | tf_op jit(solution)/shard_map/psum | solution.py:139
  469.1 1.6 broadcast_multiply_fusion.1
  470.7 1.6 multiply_bitcast_fusion
  (280 shorter events, 14.5 us)
Async XLA Ops:
  7.2 106.0 %copy-start = (bf16[100,512]{1,0:T(8,128)(2,1)S(1)}, bf16[100,512]{1,0:T(8,128)(2,1)}, u32[]{:S(2)}) copy-start(bf16[100,512]{1,0:T(8,128)(2,1)} %param.14) | copy-start | bytes 307204
  7.2 461.9 %all-reduce.8.cloned.1.call-start = ((), (), s32[]{:S(2)}) async-start(), calls=%async_computation | async-start | bytes 851968 | tf_op jit(solution)/shard_map/psum | solution.py:139
  9.1 7.6 %collective-permute-start = (f32[101,1,128]{2,1,0:T(1,128)S(1)}, f32[101,1,128]{2,1,0:T(1,128)S(1)}, u32[]{:S(2)}, u32[]{:S(2)}) collective-permute-start(f32[101,1,128]{2,1,0:T(1,128)S(1)} %get-tuple-element.624), channel_id=1, source_target_pairs={{0,32},{32,64},{64,96},{96,128},{128,160},{160,192},{192,224},{224... | collective-permute-start | bytes 155144 | tf_op jit(solution)/shard_map/ppermute | solution.py:18
  11.3 5.4 %collective-permute-start.1 = (f32[101,1,128]{2,1,0:T(1,128)S(1)}, f32[101,1,128]{2,1,0:T(1,128)S(1)}, u32[]{:S(2)}, u32[]{:S(2)}) collective-permute-start(f32[101,1,128]{2,1,0:T(1,128)S(1)} %get-tuple-element.625), channel_id=1, source_target_pairs={{32,0},{64,32},{96,64},{128,96},{160,128},{192,160},{224,192},{0,2... | collective-permute-start | bytes 155144 | tf_op jit(solution)/shard_map/ppermute | solution.py:21
  18.2 8.5 %copy-start.1 = (f32[100,8,128]{2,1,0:T(8,128)S(1)}, f32[100,8,128]{2,1,0:T(8,128)}, u32[]{:S(2)}) copy-start(f32[100,8,128]{2,1,0:T(8,128)} %param.9) | copy-start | bytes 1228804
  18.6 4.1 collective-permute-start.2
  22.2 3.1 collective-permute-start.3
  25.8 0.9 copy-start.2
  26.7 1.2 copy-start.11
  27.2 0.8 copy-start.4
  27.9 85.2 %copy-start.13 = (f32[512]{0:T(512)S(1)}, f32[512]{0:T(512)}, u32[]{:S(2)}) copy-start(f32[512]{0:T(512)} %param.15) | copy-start | bytes 6148
  113.2 2.0 copy-start.12
  113.2 1.9 copy-start.14
  115.1 1.0 copy-start.9
  115.1 1.1 copy-start.5
  116.5 1.1 copy-start.3
  120.4 2.4 copy-start.7
  127.4 2.0 copy-start.6
  128.4 1.0 copy-start.10
  133.0 80.4 %collective-permute-start.4 = (f32[100,1,128]{2,1,0:T(1,128)S(1)}, f32[100,1,128]{2,1,0:T(1,128)S(1)}, u32[]{:S(2)}, u32[]{:S(2)}) collective-permute-start(f32[100,1,128]{2,1,0:T(1,128)S(1)} %get-tuple-element.627), channel_id=1, source_target_pairs={{32,0},{64,32},{96,64},{128,96},{160,128},{192,160},{224,192},{0,2... | collective-permute-start | bytes 153608 | tf_op jit(solution)/shard_map/ppermute | solution.py:21
  135.2 78.2 %collective-permute-start.5 = (f32[100,1,128]{2,1,0:T(1,128)S(1)}, f32[100,1,128]{2,1,0:T(1,128)S(1)}, u32[]{:S(2)}, u32[]{:S(2)}) collective-permute-start(f32[100,1,128]{2,1,0:T(1,128)S(1)} %get-tuple-element.626), channel_id=1, source_target_pairs={{0,32},{32,64},{64,96},{96,128},{128,160},{160,192},{192,224},{224... | collective-permute-start | bytes 153608 | tf_op jit(solution)/shard_map/ppermute | solution.py:18
  216.2 4.2 collective-permute-start.6
  219.0 3.1 collective-permute-start.7
  220.4 3.0 copy-start.8
Sparse Core Ops, SparseCore 0:
  220.6 248.5 all-reduce.7
where the time goes:
time: 480 us; the launch traced here: 479 us
  waiting for transfers between devices  248 us (52%)
  blocking collectives  158 us (33%)
  other arithmetic  22.1 us (5%)
  between operations  15.9 us (3%)
  starting transfers between devices  14.3 us (3%)
  local copies, waits for them, and re-layouts  12.6 us (3%)
  matrix products  8.1 us (2%)
    psum x1, waiting for transfers between devices, shards(): lax.psum((grad_in, grad_out_t, grad_bin, grad_bout, level_part), ('lat',...  243 us
    psum x1, blocking collectives, shards(): energy = lax.psum(jnp.sum(wet_tracer * wet_tracer, axis=1), ('lat', 'lon'))  82 us
    psum x1, blocking collectives, shards(): lax.psum((grad_in, grad_out_t, grad_bin, grad_bout, level_part), ('lat',...  76.5 us
  transfers between devices with their start and end apart: 9, of which 5 were waited for; matrix products, arithmetic and copies ran while one was open for 2% of the time, Pallas kernels for 0%

commit v1 on v0

v1 whole, which is shorter than its diff:
```python
import functools
import math

import jax
import jax.numpy as jnp
from jax import lax
from jax.experimental import pallas as pl
from jax.experimental.pallas import tpu as pltpu
from jax.sharding import PartitionSpec as P

MESH = pl.DeviceIdType.MESH
F32 = jnp.float32
BF16 = jnp.bfloat16

spread_coef = 0.15
level_eps = 1e-05

LEVELS = 100
ROWS = 8
LANES = 128
HIDDEN = 512
COLS = ROWS * LANES
PAD = 104
LAT = 8
LON = 32
PLANE = 32
DEPTH = 8


def split_lon(lon):
    return lon // 16, (lon // 2) % 8, lon % 2


def plane_peer(q, z):
    return q // 4, ((q // 2) % 2) * 16 + z * 2 + q % 2


def z_peer(z, lat, lon_hi, core):
    return lat, lon_hi * 16 + z * 2 + core


def kernel(
    tracer_hbm, cot_hbm, land_ref, bottom_ref, kappa_s, w_in_ref, b_in_ref, w_out_ref, b_out_s,
    out_ref, gw_in_ref, gb_in_ref, gw_out_ref, gb_out_ref,
    tr_v, cot_v, slabs, adj_slabs, edge_hi, edge_lo, edge2_hi, edge2_lo,
    halo, halo2, near_depth,
    small_src, small_r1, small_mid, small_r2,
    small2_src, small2_r1, small2_mid, small2_r2,
    wi_f, wo_f, wi_b, w1t, wot, wo_b,
    inp, hid, slope, dpre, dlog, din,
    logit, mixed, val_x, val_y, mul_x, mul_y, gate, adj, dlev,
    g_in, g_out, ra_in, ra_out, mid_in, mid_out, rz_in, rz_out, ch_in, ch_out, fin_in, fin_out,
    load_sems, send_sems, recv_sems, halo_send, halo_recv,
):
    lat = lax.axis_index("lat")
    lon = lax.axis_index("lon")
    lon_hi, z_me, core = split_lon(lon)
    q_me = lat * 4 + lon_hi * 2 + core

    load_tr = pltpu.make_async_copy(tracer_hbm, tr_v, load_sems.at[0])
    load_tr.start()
    load_cot = pltpu.make_async_copy(cot_hbm, cot_v, load_sems.at[1])
    load_cot.start()

    def plane_id(d):
        q = (q_me + d) % PLANE
        return q, plane_peer(q, z_me)

    def z_id(d):
        z = (z_me + d) % DEPTH
        return z, z_peer(z, lat, lon_hi, core)

    barrier = pltpu.get_barrier_semaphore()

    def greet_plane(d, carry):
        _, dev = plane_id(d)
        pl.semaphore_signal(barrier, inc=1, device_id=dev, device_id_type=MESH)
        return carry

    def greet_z(d, carry):
        _, dev = z_id(d)
        pl.semaphore_signal(barrier, inc=1, device_id=dev, device_id_type=MESH)
        return carry

    lax.fori_loop(1, PLANE, greet_plane, 0)
    lax.fori_loop(1, DEPTH, greet_z, 0)
    far_lon = (lon + 2 * core - 1 + LON) % LON
    pl.semaphore_signal(barrier, inc=1, device_id=(lat, far_lon), device_id_type=MESH)

    row_id = lax.broadcasted_iota(jnp.int32, (PAD, LANES), 0)
    lane_id = lax.broadcasted_iota(jnp.int32, (PAD, LANES), 1)
    row_f = row_id.astype(F32)
    diag = row_id == lane_id

    def as_row(column):
        return jnp.sum(jnp.where(diag, column, 0.0), axis=0, keepdims=True)

    def as_column(row):
        return jnp.sum(jnp.where(diag, row, 0.0), axis=1, keepdims=True)

    depth_all = (land_ref[...] * bottom_ref[...]).astype(F32)

    load_tr.wait()
    energy = jnp.zeros((PAD, LANES), F32)
    hi = jnp.zeros((PAD, LANES), F32)
    lo = jnp.zeros((PAD, LANES), F32)
    for i in range(ROWS):
        slabs[i, 0:LEVELS, :] = tr_v[:, i, :]
        slabs[i, LEVELS:PAD, :] = jnp.broadcast_to(depth_all[i : i + 1, :], (PAD - LEVELS, LANES))
        x = slabs[i]
        wet_x = jnp.where(row_f < depth_all[i : i + 1, :], x, 0.0)
        energy = energy + wet_x * wet_x
        hi = jnp.where(lane_id == i, pltpu.roll(x, i + 1, 1), hi)
        lo = jnp.where(lane_id == i, pltpu.roll(x, i, 1) if i else x, lo)
    edge_hi[...] = hi
    edge_lo[...] = lo
    small_src[...] = as_row(jnp.sum(energy, axis=1, keepdims=True))
    small_r1[q_me] = small_src[...]

    pl.semaphore_wait(barrier, PLANE - 1 + DEPTH - 1 + 1)

    def small_plane(src, dst, which):
        def send(d, carry):
            _, dev = plane_id(d)
            pltpu.make_async_remote_copy(
                src, dst.at[q_me], send_sems.at[which], recv_sems.at[which],
                device_id=dev, device_id_type=MESH,
            ).start()
            return carry

        lax.fori_loop(1, PLANE, send, 0)

    def small_z(src, dst, which):
        def send(d, carry):
            _, dev = z_id(d)
            pltpu.make_async_remote_copy(
                src, dst.at[z_me], send_sems.at[which], recv_sems.at[which],
                device_id=dev, device_id_type=MESH,
            ).start()
            return carry

        lax.fori_loop(1, DEPTH, send, 0)

    def drain(ref, sem):
        pltpu.make_async_copy(ref, ref, sem).wait()

    def send_halo(k, pieces, dst):
        up = (lat + 1) % LAT
        down = (lat + LAT - 1) % LAT
        right = (lon + 1) % LON
        left = (lon + LON - 1) % LON
        targets = ((up, lon), (down, lon), (lat, right), (lat, left))
        copies = []
        for n, (src, dev) in enumerate(zip(pieces, targets)):
            copy = pltpu.make_async_remote_copy(
                src, dst.at[n], halo_send.at[4 * k + n], halo_recv.at[4 * k + n],
                device_id=dev, device_id_type=MESH,
            )
            copy.start()
            copies.append(copy)
        return copies

    small_plane(small_src, small_r1, 0)
    halo_copies = send_halo(0, (slabs.at[ROWS - 1], slabs.at[0], edge_hi, edge_lo), halo)

    bias = b_in_ref[...]
    bias_hi = bias.astype(BF16).astype(F32)
    bias_mid = (bias - bias_hi).astype(BF16).astype(F32)
    bias_lo = bias - bias_hi - bias_mid
    wi_f[LEVELS:LANES, :] = jnp.zeros((LANES - LEVELS, HIDDEN), F32)
    wi_f[0:LEVELS, :] = w_in_ref[...].astype(F32)
    wi_f[LEVELS : LEVELS + 1, :] = bias_hi
    wi_f[LEVELS + 1 : LEVELS + 2, :] = bias_mid
    wi_f[LEVELS + 2 : LEVELS + 3, :] = bias_lo
    wi_b[...] = wi_f[...].astype(BF16)
    w1t[...] = wi_f[...].T.astype(BF16)
    wo_f[...] = jnp.zeros((HIDDEN, LANES), F32)
    wo_f[:, 0:LEVELS] = w_out_ref[...].astype(F32)
    wo_b[...] = wo_f[...].astype(BF16)
    wot[...] = wo_f[...].T.astype(BF16)
    dlev[LEVELS:LANES] = jnp.zeros((LANES - LEVELS, ROWS, LANES), F32)

    drain(small_r1.at[pl.ds(0, PLANE - 1)], recv_sems.at[0])
    small_mid[...] = jnp.sum(small_r1[...], axis=0)
    small_r2[z_me] = small_mid[...]
    small_z(small_mid, small_r2, 1)

    for copy in halo_copies:
        copy.wait_recv()

    def neighbours(field, edges, i):
        centre = field[i]
        below = field[i + 1] if i + 1 < ROWS else edges[1]
        above = field[i - 1] if i else edges[0]
        from_left = pltpu.roll(edges[2], LANES - i, 1) if i else edges[2]
        left = jnp.where(lane_id == 0, from_left, pltpu.roll(centre, 1, 1))
        right = jnp.where(
            lane_id == LANES - 1, pltpu.roll(edges[3], LANES - 1 - i, 1), pltpu.roll(centre, LANES - 1, 1)
        )
        return centre, (below, above, left, right)

    def flux(centre, near, i):
        total = jnp.zeros((PAD, LANES), F32)
        for n in range(4):
            total = total + jnp.where(
                row_f < near_depth[n * ROWS + i : n * ROWS + i + 1, :], near[n] - centre, 0.0
            )
        return centre + spread_coef * total

    has_above = jnp.where(lat > 0, 1.0, 0.0)
    has_below = jnp.where(lat < LAT - 1, 1.0, 0.0)
    for i in range(ROWS):
        centre, near = neighbours(slabs, halo, i)
        own = centre[LEVELS : LEVELS + 1, :]
        for n in range(4):
            other = near[n][LEVELS : LEVELS + 1, :]
            if n == 0 and i == ROWS - 1:
                other = other * has_below
            if n == 1 and i == 0:
                other = other * has_above
            near_depth[n * ROWS + i : n * ROWS + i + 1, :] = jnp.minimum(own, other)
        mixed[:, i, :] = flux(centre, near, i)[0:LEVELS]

    drain(small_r2.at[pl.ds(0, DEPTH - 1)], recv_sems.at[1])
    energy_all = as_column(jnp.sum(small_r2[...], axis=0))
    count = float(LAT * LON * COLS)
    radius = jnp.sqrt(energy_all / count + level_eps)
    inv_radius = 1.0 / radius

    def wet_slab(i):
        x = slabs[i]
        return jnp.where(row_f < x[LEVELS : LEVELS + 1, :], x, 0.0)

    inp[PAD - 8 : LANES, :] = jnp.zeros((LANES - PAD + 8, COLS), BF16)
    one_rows = jnp.where(row_id < LEVELS + 3, 1.0, 0.0)
    for i in range(ROWS):
        scaled = jnp.where(row_id < LEVELS, wet_slab(i) * inv_radius, one_rows)
        scaled = jnp.concatenate([scaled, jnp.zeros((LANES - PAD, LANES), F32)], axis=0)
        inp[:, i * LANES : (i + 1) * LANES] = scaled.astype(BF16)

    width = 256
    for j in range(COLS // width):
        cols = slice(j * width, (j + 1) * width)
        pre = jnp.dot(w1t[...], inp[:, cols], preferred_element_type=F32)
        sig = 1.0 / (1.0 + jnp.exp(-pre))
        act = pre * sig
        hid[:, cols] = act.astype(BF16)
        slope[:, cols] = sig * (1.0 + pre * (1.0 - sig))
        out = jnp.dot(wot[...], hid[:, cols], preferred_element_type=F32)
        for s in range(width // LANES):
            logit[:, j * (width // LANES) + s, :] = out[0:LEVELS, s * LANES : (s + 1) * LANES]

    load_cot.wait()
    depth = depth_all
    half = LEVELS // 2

    def level_terms(k):
        x = logit[k] + b_out_s[k]
        ex = jnp.exp(-jnp.abs(x))
        soft = jnp.maximum(x, 0.0) + jnp.log1p(ex)
        sig = jnp.where(x >= 0.0, 1.0, ex) / (1.0 + ex)
        kf = (k + 1).astype(F32)
        open_face = kf < depth
        kap = kappa_s[k]
        down = jnp.where(open_face, kap + soft, 0.0)
        up = jnp.where(open_face, kap, 0.0)
        gate[k] = jnp.where(open_face, sig, 0.0)
        return down, up

    def eliminate(s, carry):
        down_p, up_p, r_p, v_p, w_p, sb_n, u_n, z_n = carry
        k = s
        down, up = level_terms(k)
        pivot = 1.0 + down + up_p - down_p * up_p * r_p
        r = 1.0 / pivot
        v = (mixed[k] + down_p * v_p) * r
        w = (cot_v[k] + up_p * w_p) * r
        val_x[k] = v
        val_y[k] = w
        mul_x[k] = up * r
        mul_y[k] = down * r
        b = LEVELS - 1 - s
        down_b, up_b = level_terms(b)
        up_above = jnp.where(b.astype(F32) < depth, kappa_s[b - 1], 0.0)
        pivot_b = 1.0 + down_b + up_above - down_b * up_b * sb_n
        sb = 1.0 / pivot_b
        u = (mixed[b] + up_b * u_n) * sb
        zz = (cot_v[b] + down_b * z_n) * sb
        val_x[b] = u
        val_y[b] = zz
        mul_y[b] = up_above * sb
        mul_x[b + 1] = down_b * sb_n
        return down, up, r, v, w, sb, u, zz

    zero = jnp.zeros((ROWS, LANES), F32)
    down_m, up_m, r_m, v_m, w_m, sb_m, u_m, z_m = lax.fori_loop(
        0, half, eliminate, (zero,) * 8, unroll=5
    )
    ratio_x = up_m * r_m
    ratio_y = down_m * r_m
    back_x = down_m * sb_m
    back_y = up_m * sb_m
    inv_det = 1.0 / (1.0 - ratio_x * back_x)
    x_top = (v_m + ratio_x * u_m) * inv_det
    x_bot = u_m + back_x * x_top
    y_top = (w_m + ratio_y * z_m) * inv_det
    y_bot = z_m + back_y * y_top
    adj[half - 1] = y_top
    adj[half] = y_bot
    dlev[half - 1] = gate[half - 1] * x_top * (y_bot - y_top)

    def substitute(s, carry):
        x_t, y_t, x_b, y_b = carry
        k = half - 1 - s
        x_n = val_x[k] + mul_x[k] * x_t
        y_n = val_y[k] + mul_y[k] * y_t
        adj[k] = y_n
        dlev[k] = gate[k] * x_n * (y_t - y_n)
        b = half + s
        x_c = val_x[b] + mul_x[b] * x_b
        y_c = val_y[b] + mul_y[b] * y_b
        adj[b] = y_c
        dlev[b - 1] = gate[b - 1] * x_b * (y_c - y_b)
        return x_n, y_n, x_c, y_c

    lax.fori_loop(1, half, substitute, (x_top, y_top, x_bot, y_bot), unroll=7)
    dlev[LEVELS - 1] = zero

    hi = jnp.zeros((LEVELS, LANES), F32)
    lo = jnp.zeros((LEVELS, LANES), F32)
    lane_l = lane_id[0:LEVELS]
    for i in range(ROWS):
        x = adj[:, i, :]
        adj_slabs[i, 0:LEVELS, :] = x
        hi = jnp.where(lane_l == i, pltpu.roll(x, i + 1, 1), hi)
        lo = jnp.where(lane_l == i, pltpu.roll(x, i, 1) if i else x, lo)
    edge2_hi[0:LEVELS, :] = hi
    edge2_lo[0:LEVELS, :] = lo
    for i in range(ROWS):
        adj_slabs[i, LEVELS:PAD, :] = jnp.zeros((PAD - LEVELS, LANES), F32)
    edge2_hi[LEVELS:PAD, :] = jnp.zeros((PAD - LEVELS, LANES), F32)
    edge2_lo[LEVELS:PAD, :] = jnp.zeros((PAD - LEVELS, LANES), F32)
    for i in range(ROWS):
        dlog[:, i * LANES : (i + 1) * LANES] = dlev[:, i, :].astype(BF16)
    halo2_copies = send_halo(
        1, (adj_slabs.at[ROWS - 1], adj_slabs.at[0], edge2_hi, edge2_lo), halo2
    )

    contract_last = (((1,), (1,)), ((), ()))
    grad_out = lax.dot_general(hid[...], dlog[...], contract_last, preferred_element_type=F32)
    g_out[...] = grad_out.reshape(PLANE, HIDDEN // PLANE, LANES)
    ra_out[q_me] = g_out[q_me]
    bout_row = lax.dot_general(
        jnp.ones((16, COLS), BF16), dlog[...], contract_last, preferred_element_type=F32
    )[0:1]

    def scatter(src, dst, which):
        def send(d, carry):
            q, dev = plane_id(d)
            pltpu.make_async_remote_copy(
                src.at[q], dst.at[q_me], send_sems.at[which], recv_sems.at[which],
                device_id=dev, device_id_type=MESH,
            ).start()
            return carry

        lax.fori_loop(1, PLANE, send, 0)

    def gather(src, dst, which):
        small_plane(src, dst, which)

    scatter(g_out, ra_out, 2)

    for j in range(COLS // width):
        cols = slice(j * width, (j + 1) * width)
        back = jnp.dot(wo_b[...], dlog[:, cols], preferred_element_type=F32)
        dpre[:, cols] = (back * slope[:, cols]).astype(BF16)
    grad_in = lax.dot_general(inp[...], dpre[...], contract_last, preferred_element_type=F32)
    for p in range(PLANE // 2):
        g_in[2 * p] = grad_in[8 * p : 8 * p + 8, 0:256]
        g_in[2 * p + 1] = grad_in[8 * p : 8 * p + 8, 256:512]
    ra_in[q_me] = g_in[q_me]
    scatter(g_in, ra_in, 3)

    level = jnp.zeros((PAD, LANES), F32)
    for j in range(COLS // width):
        cols = slice(j * width, (j + 1) * width)
        out = jnp.dot(wi_b[...], dpre[:, cols], preferred_element_type=F32)
        for s in range(width // LANES):
            i = j * (width // LANES) + s
            part = out[0:PAD, s * LANES : (s + 1) * LANES]
            din[i] = part
            level = level + part * wet_slab(i)
    small2_src[:, 0:LANES] = as_row(jnp.sum(level, axis=1, keepdims=True))
    small2_src[:, LANES : 2 * LANES] = bout_row
    small2_r1[q_me] = small2_src[...]
    small_plane(small2_src, small2_r1, 4)

    drain(ra_out.at[pl.ds(0, PLANE - 1)], recv_sems.at[2])
    mid_out[...] = jnp.sum(ra_out[...], axis=0)
    rz_out[z_me] = mid_out[...]
    small_z(mid_out, rz_out, 5)
    drain(ra_in.at[pl.ds(0, PLANE - 1)], recv_sems.at[3])
    mid_in[...] = jnp.sum(ra_in[...], axis=0)
    rz_in[z_me] = mid_in[...]
    small_z(mid_in, rz_in, 6)
    drain(small2_r1.at[pl.ds(0, PLANE - 1)], recv_sems.at[4])
    small2_mid[...] = jnp.sum(small2_r1[...], axis=0)
    small2_r2[z_me] = small2_mid[...]
    small_z(small2_mid, small2_r2, 7)

    scale = 1.0 / math.sqrt(count)
    drain(rz_out.at[pl.ds(0, DEPTH - 1)], recv_sems.at[5])
    ch_out[...] = jnp.sum(rz_out[...], axis=0) * scale
    fin_out[q_me] = ch_out[...]
    gather(ch_out, fin_out, 8)
    drain(rz_in.at[pl.ds(0, DEPTH - 1)], recv_sems.at[6])
    ch_in[...] = jnp.sum(rz_in[...], axis=0) * scale
    fin_in[q_me] = ch_in[...]
    gather(ch_in, fin_in, 9)

    for copy in halo2_copies:
        copy.wait_recv()
    drain(small2_r2.at[pl.ds(0, DEPTH - 1)], recv_sems.at[7])
    small2 = jnp.sum(small2_r2[...], axis=0)
    level_sum = as_column(small2[:, 0:LANES])
    gb_out_ref[...] = small2[:, LANES : 2 * LANES] * scale
    level_scale = level_sum / (count * radius * radius * radius)
    for i in range(ROWS):
        centre, near = neighbours(adj_slabs, halo2, i)
        mix = flux(centre, near, i)
        x = slabs[i]
        wet = row_f < x[LEVELS : LEVELS + 1, :]
        total = mix + jnp.where(wet, din[i] * inv_radius - x * level_scale, 0.0)
        out_ref[:, i, :] = total[0:LEVELS]

    drain(fin_out.at[pl.ds(0, PLANE - 1)], recv_sems.at[8])
    gw_out_ref[...] = fin_out[...].reshape(HIDDEN, LANES)[:, 0:LEVELS]
    drain(fin_in.at[pl.ds(0, PLANE - 1)], recv_sems.at[9])
    for p in range(LEVELS // 8 + 1):
        rows = min(8, LEVELS - 8 * p)
        gw_in_ref[8 * p : 8 * p + rows, 0:256] = fin_in[2 * p, 0:rows, :]
        gw_in_ref[8 * p : 8 * p + rows, 256:512] = fin_in[2 * p + 1, 0:rows, :]
    bias_tile, bias_row = LEVELS // 8, LEVELS % 8
    gb_in_ref[:, 0:256] = fin_in[2 * bias_tile, bias_row : bias_row + 1, :]
    gb_in_ref[:, 256:512] = fin_in[2 * bias_tile + 1, bias_row : bias_row + 1, :]

    for copy in halo_copies + halo2_copies:
        copy.wait_send()
    drain(small_r1.at[pl.ds(0, PLANE - 1)], send_sems.at[0])
    drain(small_r2.at[pl.ds(0, DEPTH - 1)], send_sems.at[1])
    drain(ra_out.at[pl.ds(0, PLANE - 1)], send_sems.at[2])
    drain(ra_in.at[pl.ds(0, PLANE - 1)], send_sems.at[3])
    drain(small2_r1.at[pl.ds(0, PLANE - 1)], send_sems.at[4])
    drain(rz_out.at[pl.ds(0, DEPTH - 1)], send_sems.at[5])
    drain(rz_in.at[pl.ds(0, DEPTH - 1)], send_sems.at[6])
    drain(small2_r2.at[pl.ds(0, DEPTH - 1)], send_sems.at[7])
    drain(fin_out.at[pl.ds(0, PLANE - 1)], send_sems.at[8])
    drain(fin_in.at[pl.ds(0, PLANE - 1)], send_sems.at[9])


def shards(tracer, cotangent, land_mask, bottom, kappa, w_in, b_in, w_out, b_out):
    vmem = pl.BlockSpec(memory_space=pltpu.VMEM)
    smem = pl.BlockSpec(memory_space=pltpu.SMEM)
    anyw = pl.BlockSpec(memory_space=pl.ANY)
    slab = (ROWS, PAD, LANES)
    levels = (LEVELS, ROWS, LANES)

    def v(*shape, dtype=F32):
        return pltpu.VMEM(shape, dtype)

    scratch = [
        v(*levels), v(*levels), v(*slab), v(*slab),
        v(PAD, LANES), v(PAD, LANES), v(PAD, LANES), v(PAD, LANES),
        v(4, PAD, LANES), v(4, PAD, LANES), v(4 * ROWS, LANES),
        v(1, LANES), v(PLANE, 1, LANES), v(1, LANES), v(DEPTH, 1, LANES),
        v(1, 2 * LANES), v(PLANE, 1, 2 * LANES), v(1, 2 * LANES), v(DEPTH, 1, 2 * LANES),
        v(LANES, HIDDEN), v(HIDDEN, LANES), v(LANES, HIDDEN, dtype=BF16),
        v(HIDDEN, LANES, dtype=BF16), v(LANES, HIDDEN, dtype=BF16), v(HIDDEN, LANES, dtype=BF16),
        v(LANES, COLS, dtype=BF16), v(HIDDEN, COLS, dtype=BF16), v(HIDDEN, COLS),
        v(HIDDEN, COLS, dtype=BF16), v(LANES, COLS, dtype=BF16), v(*slab),
        v(*levels), v(*levels), v(*levels), v(*levels), v(LEVELS + 1, ROWS, LANES),
        v(*levels), v(*levels), v(*levels), v(LANES, ROWS, LANES),
        v(PLANE, 8, 256), v(PLANE, 16, LANES), v(PLANE, 8, 256), v(PLANE, 16, LANES),
        v(8, 256), v(16, LANES), v(DEPTH, 8, 256), v(DEPTH, 16, LANES),
        v(8, 256), v(16, LANES), v(PLANE, 8, 256), v(PLANE, 16, LANES),
        pltpu.SemaphoreType.DMA((2,)), pltpu.SemaphoreType.DMA((10,)),
        pltpu.SemaphoreType.DMA((10,)), pltpu.SemaphoreType.DMA((8,)),
        pltpu.SemaphoreType.DMA((8,)),
    ]
    out, gw_in, gb_in, gw_out, gb_out = pl.pallas_call(
        kernel,
        out_shape=(
            jax.ShapeDtypeStruct(tracer.shape, F32),
            jax.ShapeDtypeStruct((LEVELS, HIDDEN), F32),
            jax.ShapeDtypeStruct((1, HIDDEN), F32),
            jax.ShapeDtypeStruct((HIDDEN, LEVELS), F32),
            jax.ShapeDtypeStruct((1, LANES), F32),
        ),
        in_specs=[anyw, anyw, vmem, vmem, smem, vmem, vmem, vmem, smem],
        out_specs=(vmem,) * 5,
        scratch_shapes=scratch,
        compiler_params=pltpu.CompilerParams(
            collective_id=0, has_side_effects=True, vmem_limit_bytes=40 * 1024 * 1024
        ),
        name="step_adjoint",
    )(
        tracer, cotangent, land_mask, bottom, kappa, w_in, b_in.reshape(1, HIDDEN), w_out, b_out
    )
    return out, gw_in, gb_in[0], gw_out, gb_out[0, :LEVELS]


def solution(mesh):
    placed = (
        P(None, "lat", "lon"),
        P(None, "lat", "lon"),
        P("lat", "lon"),
        P("lat", "lon"),
        P(),
        P(),
        P(),
        P(),
        P(),
    )
    return jax.shard_map(
        shards,
        mesh=mesh,
        in_specs=placed,
        out_specs=(P(None, "lat", "lon"), P(), P(), P(), P()),
        check_vma=False,
    )
```

time: 480 us -> 55.3 us (0.12)
  waiting for transfers between devices: 248 us -> 0 us
  blocking collectives: 158 us -> 0 us
  Pallas kernels: 0 us -> 47.9 us
  other arithmetic: 22.1 us -> 0 us
  between operations: 15.9 us -> 0.74 us
  starting transfers between devices: 14.3 us -> 0 us
  matrix products: 8.1 us -> 0 us
  local copies, waits for them, and re-layouts: 12.6 us -> 6.47 us
    psum x1 -> x0, waiting for transfers between devices: 243 us -> none  [shards(): lax.psum((grad_in, grad_out_t, grad_bin, grad_bout, level_part), ('lat',...]
    psum x2 -> x0, blocking collectives: 158 us -> none  [the longest x1 82 us: shards(): energy = lax.psum(jnp.sum(wet_tracer * wet_tracer, axis=1), ('lat', 'lon'))]
    pallas_call x0 -> x1, Pallas kernels: none -> 47.9 us  [shards(): pl.pallas_call(kernel, out_shape=(jax.ShapeDtypeStruct(tracer.shape, F32)...]
    ppermute x8 -> x0, starting transfers between devices: 14.3 us -> none  [the longest x4 7.82 us: with_halo(): lax.ppermute(lax.slice_in_dim(block, block.shape[dim] - width, None, axis...]
    dot_general x6 -> x0, matrix products: 8.1 us -> none  [the longest x1 2.52 us: shards(): d_inputs = jnp.dot(w_in, d_pre, preferred_element_type=jnp.float32)]
    ppermute x8 -> x0, waiting for transfers between devices: 4.94 us -> none  [the longest x4 3.37 us: with_halo(): lax.ppermute(lax.slice_in_dim(block, 0, width, axis=dim), axis, backward)]
  transfers between devices with their start and end apart: 9 -> 0, of which waited for: 5 -> 0; matrix products, arithmetic and copies ran while one was open for 2% -> 0% of each run, Pallas kernels for 0% -> 0%
where the time goes in v1:
time: 55.3 us; the launch traced here: 55.2 us
  Pallas kernels  47.9 us (87%)
  local copies, waits for them, and re-layouts  6.47 us (12%)
  between operations  0.74 us (1%)
    pallas_call x1, Pallas kernels, shards(): pl.pallas_call(kernel, out_shape=(jax.ShapeDtypeStruct(tracer.shape, F32)...  47.9 us
    unnamed x21, local copies, waits for them, and re-layouts  5.96 us

profile of v1, /device:TPU:1, one launch (start us, length us, event | category | flops | bytes accessed | tf_op | source)
XLA Modules:
  0.0 55.2 jit_solution(14477457472400796861)
XLA Ops:
  0.6 0.0 copy-start.2
  0.6 0.0 copy-start.3
  0.7 0.0 copy-start.4
  0.7 0.0 copy-start.5
  0.7 0.0 copy-start.6
  0.7 0.0 copy-start.7
  0.7 1.1 %copy.14.w_out_ref = bf16[512,100]{1,0:T(8,128)(2,1)S(1)} copy(bf16[512,100]{0,1:T(8,128)(2,1)} %param.16) | data formatting | bytes 204800 | tf_op args[7]
  1.8 0.0 copy-done.2
  1.8 0.0 copy-done.3
  1.8 0.0 copy-done.4
  1.8 0.0 copy-done.5
  1.8 0.0 copy-done.6
  1.8 0.0 copy-done.7
  1.9 0.0 copy-start
  1.9 1.0 %copy-done = f32[100,8,128]{2,1,0:T(8,128)S(1)} copy-done((f32[100,8,128]{2,1,0:T(8,128)S(1)}, f32[100,8,128]{2,1,0:T(8,128)}, u32[]{:S(2)}) %copy-start) | copy-done | bytes 409624
  2.9 0.0 copy-start.1
  2.9 1.0 %copy-done.1 = f32[100,8,128]{2,1,0:T(8,128)S(1)} copy-done((f32[100,8,128]{2,1,0:T(8,128)S(1)}, f32[100,8,128]{2,1,0:T(8,128)}, u32[]{:S(2)}) %copy-start.1) | copy-done | bytes 409624
  3.9 47.9 %step_adjoint.1 = (f32[100,8,128]{2,1,0:T(8,128)S(1)}, f32[100,512]{1,0:T(8,128)S(1)}, f32[1,512]{1,0:T(1,128)S(1)}, f32[512,100]{1,0:T(8,128)S(1)}, f32[1,128]{1,0:T(1,128)S(1)}) custom-call(f32[100,8,128]{2,1,0:T(8,128)S(1)} %copy-done, f32[100,8,128]{2,1,0:T(8,128)S(1)} %copy-done.1, s32[8,128]{1,0:T(8,128)S(1)} %copy-done.3, s32[8,128]{1,0:T(8,128)S(1)} %copy-done.4, ...), custom_call_target="tpu_custom_call" | custom-call | tf_op jit(solution)/shard_map/step_adjoint/pallas_call | solution.py:490
  51.8 0.5 slice_bitcast_fusion
  52.3 0.8 %copy.15 = f32[512,100]{0,1:T(8,128)} copy(f32[512,100]{1,0:T(8,128)S(1)} %get-tuple-element.18) | data formatting | bytes 409600
  53.1 0.8 %copy.19 = f32[100,8,128]{2,1,0:T(8,128)} copy(f32[100,8,128]{2,1,0:T(8,128)S(1)} %get-tuple-element.25) | data formatting | bytes 819200
  53.9 0.7 %copy.20 = f32[100,512]{1,0:T(8,128)} copy(f32[100,512]{1,0:T(8,128)S(1)} %get-tuple-element.26) | data formatting | bytes 409600
  54.6 0.6 %copy.21 = f32[512]{0:T(512)} copy(f32[512]{0:T(512)S(1)} %bitcast.5) | data formatting | bytes 4096
Async XLA Ops:
  0.6 1.2 %copy-start.2 = (bf16[100,512]{1,0:T(8,128)(2,1)S(1)}, bf16[100,512]{1,0:T(8,128)(2,1)}, u32[]{:S(2)}) copy-start(bf16[100,512]{1,0:T(8,128)(2,1)} %w_in_ref.1) | copy-start | bytes 307204
  0.6 1.2 %copy-start.3 = (s32[8,128]{1,0:T(8,128)S(1)}, s32[8,128]{1,0:T(8,128)}, u32[]{:S(2)}) copy-start(s32[8,128]{1,0:T(8,128)} %land_ref.1) | copy-start | bytes 12292
  0.7 1.2 %copy-start.4 = (s32[8,128]{1,0:T(8,128)S(1)}, s32[8,128]{1,0:T(8,128)}, u32[]{:S(2)}) copy-start(s32[8,128]{1,0:T(8,128)} %bottom_ref.1) | copy-start | bytes 12292
  0.7 1.2 %copy-start.5 = (f32[512]{0:T(512)S(1)}, f32[512]{0:T(512)}, u32[]{:S(2)}) copy-start(f32[512]{0:T(512)} %param.15) | copy-start | bytes 6148
  0.7 1.2 %copy-start.6 = (f32[100]{0:T(128)S(1)}, f32[100]{0:T(128)}, u32[]{:S(2)}) copy-start(f32[100]{0:T(128)} %kappa_s.1) | copy-start | bytes 1204
  0.7 1.2 %copy-start.7 = (f32[100]{0:T(128)S(1)}, f32[100]{0:T(128)}, u32[]{:S(2)}) copy-start(f32[100]{0:T(128)} %b_out_s.1) | copy-start | bytes 1204
  1.9 1.0 %copy-start = (f32[100,8,128]{2,1,0:T(8,128)S(1)}, f32[100,8,128]{2,1,0:T(8,128)}, u32[]{:S(2)}) copy-start(f32[100,8,128]{2,1,0:T(8,128)} %tracer_hbm.1) | copy-start | bytes 1228804
  2.9 1.0 %copy-start.1 = (f32[100,8,128]{2,1,0:T(8,128)S(1)}, f32[100,8,128]{2,1,0:T(8,128)}, u32[]{:S(2)}) copy-start(f32[100,8,128]{2,1,0:T(8,128)} %cot_hbm.1) | copy-start | bytes 1228804

commit v2 on v1

v2 whole, which is shorter than its diff:
```python
import functools
import math

import jax
import jax.numpy as jnp
from jax import lax
from jax.experimental import pallas as pl
from jax.experimental.pallas import tpu as pltpu
from jax.sharding import PartitionSpec as P

MESH = pl.DeviceIdType.MESH
F32 = jnp.float32
BF16 = jnp.bfloat16

spread_coef = 0.15
level_eps = 1e-05

LEVELS = 100
ROWS = 8
LANES = 128
HIDDEN = 512
COLS = ROWS * LANES
PAD = 104
LAT = 8
LON = 32
SIDE = 4
CHIPS = SIDE * SIDE
PLANE = 2 * CHIPS
DEPTH = 8
HALF = HIDDEN // 2


def ring(d, n):
    return min(d, n - d)


CHIP_STEPS = sorted(
    ((dx, dy) for dx in range(SIDE) for dy in range(SIDE)),
    key=lambda s: -(ring(s[0], SIDE) + ring(s[1], SIDE)),
)
Z_STEPS = sorted(range(1, DEPTH), key=lambda d: -ring(d, DEPTH))


def kernel(
    tracer_hbm, cot_hbm, land_hbm, bottom_hbm, kappa_hbm, w_in_hbm, b_in_hbm, w_out_hbm, b_out_hbm,
    out_ref, gw_in_ref, gb_in_ref, gw_out_ref, gb_out_ref,
    tr_v, cot_v, land_v, bottom_v, kappa_s, w_in_v, b_in_v, w_out_v, b_out_s,
    slabs, adj_slabs, edge_hi, edge_lo, edge2_hi, edge2_lo, halo, halo2, near_depth,
    small_src, small_r1, small_mid, small_r2,
    small2_src, small2_r1, small2_mid, small2_r2,
    wi_f, wo_f, wi_b, w1t, wot, wo_b,
    inp, hid, slope, dpre, dlog, din,
    logit, mixed, val_x, val_y, mul_x, mul_y, gate, adj, dlev,
    grad, from_core, half, from_plane, mid, from_z, chunk, full,
    load_sems, small_send, small_recv, core_send, core_recv, plane_send, plane_recv,
    z_send, z_recv, gather_send, gather_recv, fwd_send, fwd_recv, halo_send, halo_recv,
):
    lat = lax.axis_index("lat")
    lon = lax.axis_index("lon")
    y_me = lat % SIDE
    x_me = (lat // SIDE) * 2 + lon // 16
    z_me = (lon // 2) % DEPTH
    core = lon % 2
    p_me = x_me * SIDE + y_me
    q_me = p_me * 2 + core
    lon_z = z_me * 2

    loads = []
    for n, (src, dst) in enumerate(
        (
            (tracer_hbm, tr_v), (land_hbm, land_v), (bottom_hbm, bottom_v), (w_in_hbm, w_in_v),
            (b_in_hbm, b_in_v), (w_out_hbm, w_out_v), (cot_hbm, cot_v), (kappa_hbm, kappa_s),
            (b_out_hbm, b_out_s),
        )
    ):
        load = pltpu.make_async_copy(src, dst, load_sems.at[n])
        load.start()
        loads.append(load)

    xs = [(x_me + d) % SIDE for d in range(SIDE)]
    ys = [(y_me + d) % SIDE for d in range(SIDE)]

    def chip_peer(dx, dy, dc):
        to_core = core if dc == 0 else 1 - core
        dev = ((xs[dx] // 2) * SIDE + ys[dy], (xs[dx] % 2) * 16 + lon_z + to_core)
        return xs[dx] * SIDE + ys[dy], dev

    def z_peer(d):
        return (lat, (lon // 16) * 16 + ((z_me + d) % DEPTH) * 2 + core)

    everyone = [(dx, dy, dc) for dx, dy in CHIP_STEPS for dc in (0, 1) if dx or dy or dc]
    same_core = [(dx, dy) for dx, dy in CHIP_STEPS if dx or dy]
    partner = (lat, lon + 1 - 2 * core)

    barrier = pltpu.get_barrier_semaphore()

    def greet(dev):
        pl.semaphore_signal(barrier, inc=1, device_id=dev, device_id_type=MESH)

    for step in everyone:
        greet(chip_peer(*step)[1])
    for d in Z_STEPS:
        greet(z_peer(d))
    greet((lat, (lon + 2 * core - 1 + LON) % LON))

    row_id = lax.broadcasted_iota(jnp.int32, (PAD, LANES), 0)
    lane_id = lax.broadcasted_iota(jnp.int32, (PAD, LANES), 1)
    row_f = row_id.astype(F32)
    diag = row_id == lane_id

    def as_row(column):
        return jnp.sum(jnp.where(diag, column, 0.0), axis=0, keepdims=True)

    def as_column(row):
        return jnp.sum(jnp.where(diag, row, 0.0), axis=1, keepdims=True)

    for n in range(3):
        loads[n].wait()
    depth_all = (land_v[...] * bottom_v[...]).astype(F32)
    energy = jnp.zeros((PAD, LANES), F32)
    hi = jnp.zeros((PAD, LANES), F32)
    lo = jnp.zeros((PAD, LANES), F32)
    for i in range(ROWS):
        slabs[i, 0:LEVELS, :] = tr_v[:, i, :]
        slabs[i, LEVELS:PAD, :] = jnp.broadcast_to(depth_all[i : i + 1, :], (PAD - LEVELS, LANES))
        x = slabs[i]
        wet_x = jnp.where(row_f < depth_all[i : i + 1, :], x, 0.0)
        energy = energy + wet_x * wet_x
        hi = jnp.where(lane_id == i, pltpu.roll(x, i + 1, 1), hi)
        lo = jnp.where(lane_id == i, pltpu.roll(x, i, 1) if i else x, lo)
    small_src[...] = as_row(jnp.sum(energy, axis=1, keepdims=True))
    small_r1[q_me] = small_src[...]
    edge_hi[...] = hi
    edge_lo[...] = lo

    pl.semaphore_wait(barrier, PLANE - 1 + DEPTH - 1 + 1)

    def post(src, dst, dev, send, recv):
        pltpu.make_async_remote_copy(
            src, dst, send, recv, device_id=dev, device_id_type=MESH
        ).start()

    def small_plane(src, dst, which):
        for step in everyone:
            post(src, dst.at[q_me], chip_peer(*step)[1], small_send.at[which], small_recv.at[which])

    def send_z(src, dst, send, recv):
        for d in Z_STEPS:
            post(src, dst.at[z_me], z_peer(d), send, recv)

    def drain(ref, sem):
        pltpu.make_async_copy(ref, ref, sem).wait()

    def send_halo(k, pieces, dst):
        up = (lat + 1) % LAT
        down = (lat + LAT - 1) % LAT
        right = (lon + 1) % LON
        left = (lon + LON - 1) % LON
        targets = ((up, lon), (down, lon), (lat, right), (lat, left))
        copies = []
        for n, (src, dev) in enumerate(zip(pieces, targets)):
            copy = pltpu.make_async_remote_copy(
                src, dst.at[n], halo_send.at[4 * k + n], halo_recv.at[4 * k + n],
                device_id=dev, device_id_type=MESH,
            )
            copy.start()
            copies.append(copy)
        return copies

    small_plane(small_src, small_r1, 0)
    halo_copies = send_halo(0, (slabs.at[ROWS - 1], slabs.at[0], edge_hi, edge_lo), halo)

    for n in range(3, 6):
        loads[n].wait()
    bias = b_in_v[...].reshape(1, HIDDEN)
    bias_hi = bias.astype(BF16).astype(F32)
    bias_mid = (bias - bias_hi).astype(BF16).astype(F32)
    bias_lo = bias - bias_hi - bias_mid
    wi_f[LEVELS:LANES, :] = jnp.zeros((LANES - LEVELS, HIDDEN), F32)
    wi_f[0:LEVELS, :] = w_in_v[...].astype(F32)
    wi_f[LEVELS : LEVELS + 1, :] = bias_hi
    wi_f[LEVELS + 1 : LEVELS + 2, :] = bias_mid
    wi_f[LEVELS + 2 : LEVELS + 3, :] = bias_lo
    wi_b[...] = wi_f[...].astype(BF16)
    w1t[...] = wi_f[...].T.astype(BF16)
    wo_f[LEVELS:LANES, :] = jnp.zeros((LANES - LEVELS, HIDDEN), F32)
    wo_f[0:LEVELS, :] = w_out_v[...].astype(F32)
    wot[...] = wo_f[...].astype(BF16)
    wo_b[...] = wo_f[...].T.astype(BF16)
    dlev[LEVELS:LANES] = jnp.zeros((LANES - LEVELS, ROWS, LANES), F32)
    for i in range(ROWS):
        adj_slabs[i, LEVELS:PAD, :] = jnp.zeros((PAD - LEVELS, LANES), F32)
    edge2_hi[LEVELS:PAD, :] = jnp.zeros((PAD - LEVELS, LANES), F32)
    edge2_lo[LEVELS:PAD, :] = jnp.zeros((PAD - LEVELS, LANES), F32)
    inp[PAD - 8 : LANES, :] = jnp.zeros((LANES - PAD + 8, COLS), BF16)
    for n in range(6, 9):
        loads[n].wait()

    drain(small_r1.at[pl.ds(0, PLANE - 1)], small_recv.at[0])
    small_mid[...] = jnp.sum(small_r1[...], axis=0)
    small_r2[z_me] = small_mid[...]
    send_z(small_mid, small_r2, small_send.at[1], small_recv.at[1])

    for copy in halo_copies:
        copy.wait_recv()

    def neighbours(field, edges, i):
        centre = field[i]
        below = field[i + 1] if i + 1 < ROWS else edges[1]
        above = field[i - 1] if i else edges[0]
        from_left = pltpu.roll(edges[2], LANES - i, 1) if i else edges[2]
        left = jnp.where(lane_id == 0, from_left, pltpu.roll(centre, 1, 1))
        right = jnp.where(
            lane_id == LANES - 1, pltpu.roll(edges[3], LANES - 1 - i, 1), pltpu.roll(centre, LANES - 1, 1)
        )
        return centre, (below, above, left, right)

    def flux(centre, near, i):
        total = jnp.zeros((PAD, LANES), F32)
        for n in range(4):
            total = total + jnp.where(
                row_f < near_depth[n * ROWS + i : n * ROWS + i + 1, :], near[n] - centre, 0.0
            )
        return centre + spread_coef * total

    has_above = jnp.where(lat > 0, 1.0, 0.0)
    has_below = jnp.where(lat < LAT - 1, 1.0, 0.0)
    for i in range(ROWS):
        centre, near = neighbours(slabs, halo, i)
        own = centre[LEVELS : LEVELS + 1, :]
        for n in range(4):
            other = near[n][LEVELS : LEVELS + 1, :]
            if n == 0 and i == ROWS - 1:
                other = other * has_below
            if n == 1 and i == 0:
                other = other * has_above
            near_depth[n * ROWS + i : n * ROWS + i + 1, :] = jnp.minimum(own, other)
        mixed[:, i, :] = flux(centre, near, i)[0:LEVELS]

    drain(small_r2.at[pl.ds(0, DEPTH - 1)], small_recv.at[1])
    energy_all = as_column(jnp.sum(small_r2[...], axis=0))
    count = float(LAT * LON * COLS)
    radius = jnp.sqrt(energy_all / count + level_eps)
    inv_radius = 1.0 / radius

    def wet_slab(i):
        x = slabs[i]
        return jnp.where(row_f < x[LEVELS : LEVELS + 1, :], x, 0.0)

    one_rows = jnp.where(row_id < LEVELS + 3, 1.0, 0.0)
    for i in range(ROWS):
        scaled = jnp.where(row_id < LEVELS, wet_slab(i) * inv_radius, one_rows)
        scaled = jnp.concatenate([scaled, jnp.zeros((LANES - PAD, LANES), F32)], axis=0)
        inp[:, i * LANES : (i + 1) * LANES] = scaled.astype(BF16)

    width = 256
    for j in range(COLS // width):
        cols = slice(j * width, (j + 1) * width)
        pre = jnp.dot(w1t[...], inp[:, cols], preferred_element_type=F32)
        sig = 1.0 / (1.0 + jnp.exp(-pre))
        act = pre * sig
        hid[:, cols] = act.astype(BF16)
        slope[:, cols] = sig * (1.0 + pre * (1.0 - sig))
        out = jnp.dot(wot[...], hid[:, cols], preferred_element_type=F32)
        for s in range(width // LANES):
            logit[:, j * (width // LANES) + s, :] = out[0:LEVELS, s * LANES : (s + 1) * LANES]

    depth = depth_all
    middle = LEVELS // 2

    def level_terms(k):
        x = logit[k] + b_out_s[k]
        ex = jnp.exp(-jnp.abs(x))
        soft = jnp.maximum(x, 0.0) + jnp.log1p(ex)
        sig = jnp.where(x >= 0.0, 1.0, ex) / (1.0 + ex)
        kf = (k + 1).astype(F32)
        open_face = kf < depth
        kap = kappa_s[k]
        down = jnp.where(open_face, kap + soft, 0.0)
        up = jnp.where(open_face, kap, 0.0)
        gate[k] = jnp.where(open_face, sig, 0.0)
        return down, up

    def eliminate(s, carry):
        down_p, up_p, r_p, v_p, w_p, sb_n, u_n, z_n = carry
        k = s
        down, up = level_terms(k)
        pivot = 1.0 + down + up_p - down_p * up_p * r_p
        r = 1.0 / pivot
        v = (mixed[k] + down_p * v_p) * r
        w = (cot_v[k] + up_p * w_p) * r
        val_x[k] = v
        val_y[k] = w
        mul_x[k] = up * r
        mul_y[k] = down * r
        b = LEVELS - 1 - s
        down_b, up_b = level_terms(b)
        up_above = jnp.where(b.astype(F32) < depth, kappa_s[b - 1], 0.0)
        pivot_b = 1.0 + down_b + up_above - down_b * up_b * sb_n
        sb = 1.0 / pivot_b
        u = (mixed[b] + up_b * u_n) * sb
        zz = (cot_v[b] + down_b * z_n) * sb
        val_x[b] = u
        val_y[b] = zz
        mul_y[b] = up_above * sb
        mul_x[b + 1] = down_b * sb_n
        return down, up, r, v, w, sb, u, zz

    zero = jnp.zeros((ROWS, LANES), F32)
    down_m, up_m, r_m, v_m, w_m, sb_m, u_m, z_m = lax.fori_loop(
        0, middle, eliminate, (zero,) * 8, unroll=5
    )
    ratio_x = up_m * r_m
    ratio_y = down_m * r_m
    back_x = down_m * sb_m
    back_y = up_m * sb_m
    inv_det = 1.0 / (1.0 - ratio_x * back_x)
    x_top = (v_m + ratio_x * u_m) * inv_det
    x_bot = u_m + back_x * x_top
    y_top = (w_m + ratio_y * z_m) * inv_det
    y_bot = z_m + back_y * y_top
    adj[middle - 1] = y_top
    adj[middle] = y_bot
    dlev[middle - 1] = gate[middle - 1] * x_top * (y_bot - y_top)

    def substitute(s, carry):
        x_t, y_t, x_b, y_b = carry
        k = middle - 1 - s
        x_n = val_x[k] + mul_x[k] * x_t
        y_n = val_y[k] + mul_y[k] * y_t
        adj[k] = y_n
        dlev[k] = gate[k] * x_n * (y_t - y_n)
        b = middle + s
        x_c = val_x[b] + mul_x[b] * x_b
        y_c = val_y[b] + mul_y[b] * y_b
        adj[b] = y_c
        dlev[b - 1] = gate[b - 1] * x_b * (y_c - y_b)
        return x_n, y_n, x_c, y_c

    lax.fori_loop(1, middle, substitute, (x_top, y_top, x_bot, y_bot), unroll=7)
    dlev[LEVELS - 1] = zero

    for i in range(ROWS):
        dlog[:, i * LANES : (i + 1) * LANES] = dlev[:, i, :].astype(BF16)
    contract_last = (((1,), (1,)), ((), ()))

    def share(m, value):
        for p in range(CHIPS):
            for c in range(2):
                grad[m, c, p] = value[8 * p : 8 * p + 8, c * HALF : (c + 1) * HALF]
        post(grad.at[m, 1 - core], from_core.at[m], partner, core_send.at[m], core_recv.at[m])

    share(0, lax.dot_general(dlog[...], hid[...], contract_last, preferred_element_type=F32))

    hi = jnp.zeros((LEVELS, LANES), F32)
    lo = jnp.zeros((LEVELS, LANES), F32)
    lane_l = lane_id[0:LEVELS]
    for i in range(ROWS):
        x = adj[:, i, :]
        adj_slabs[i, 0:LEVELS, :] = x
        hi = jnp.where(lane_l == i, pltpu.roll(x, i + 1, 1), hi)
        lo = jnp.where(lane_l == i, pltpu.roll(x, i, 1) if i else x, lo)
    edge2_hi[0:LEVELS, :] = hi
    edge2_lo[0:LEVELS, :] = lo

    for j in range(COLS // width):
        cols = slice(j * width, (j + 1) * width)
        back = jnp.dot(wo_b[...], dlog[:, cols], preferred_element_type=F32)
        dpre[:, cols] = (back * slope[:, cols]).astype(BF16)
    share(1, lax.dot_general(inp[...], dpre[...], contract_last, preferred_element_type=F32))

    def scatter(m):
        drain(from_core.at[m], core_recv.at[m])
        half[m] = grad[m, core] + from_core[m]
        from_plane[m, p_me] = half[m, p_me]
        for dx, dy in same_core:
            p, dev = chip_peer(dx, dy, 0)
            post(half.at[m, p], from_plane.at[m, p_me], dev, plane_send.at[m], plane_recv.at[m])

    scatter(0)
    bout_row = lax.dot_general(
        jnp.ones((16, COLS), BF16), dlog[...], contract_last, preferred_element_type=F32
    )[0:1]
    level = jnp.zeros((PAD, LANES), F32)
    for j in range(COLS // width):
        cols = slice(j * width, (j + 1) * width)
        out = jnp.dot(wi_b[...], dpre[:, cols], preferred_element_type=F32)
        for s in range(width // LANES):
            i = j * (width // LANES) + s
            part = out[0:PAD, s * LANES : (s + 1) * LANES]
            din[i] = part
            level = level + part * wet_slab(i)
    small2_src[:, 0:LANES] = as_row(jnp.sum(level, axis=1, keepdims=True))
    small2_src[:, LANES : 2 * LANES] = bout_row
    small2_r1[q_me] = small2_src[...]
    scatter(1)
    small_plane(small2_src, small2_r1, 2)
    halo2_copies = send_halo(
        1, (adj_slabs.at[ROWS - 1], adj_slabs.at[0], edge2_hi, edge2_lo), halo2
    )

    def through_z(m):
        drain(from_plane.at[m, pl.ds(0, CHIPS - 1)], plane_recv.at[m])
        mid[m] = jnp.sum(from_plane[m], axis=0)
        from_z[m, z_me] = mid[m]
        send_z(mid.at[m], from_z.at[m], z_send.at[m], z_recv.at[m])

    scale = 1.0 / math.sqrt(count)

    def gather(m):
        drain(from_z.at[m, pl.ds(0, DEPTH - 1)], z_recv.at[m])
        chunk[m] = jnp.sum(from_z[m], axis=0) * scale
        full[m, core, p_me] = chunk[m]
        for dx, dy in same_core:
            _, dev = chip_peer(dx, dy, 0)
            post(chunk.at[m], full.at[m, core, p_me], dev, gather_send.at[m], gather_recv.at[m])

    def forward(m):
        drain(full.at[m, core, pl.ds(0, CHIPS - 1)], gather_recv.at[m])
        post(full.at[m, core], full.at[m, core], partner, fwd_send.at[m], fwd_recv.at[m])

    through_z(0)
    through_z(1)
    drain(small2_r1.at[pl.ds(0, PLANE - 1)], small_recv.at[2])
    small2_mid[...] = jnp.sum(small2_r1[...], axis=0)
    small2_r2[z_me] = small2_mid[...]
    send_z(small2_mid, small2_r2, small_send.at[3], small_recv.at[3])
    for copy in halo2_copies:
        copy.wait_recv()
    for i in range(ROWS):
        centre, near = neighbours(adj_slabs, halo2, i)
        mix = flux(centre, near, i)
        wet = row_f < slabs[i, LEVELS : LEVELS + 1, :]
        din[i] = mix + jnp.where(wet, din[i] * inv_radius, 0.0)
    gather(0)
    gather(1)

    drain(small2_r2.at[pl.ds(0, DEPTH - 1)], small_recv.at[3])
    small2 = jnp.sum(small2_r2[...], axis=0)
    level_sum = as_column(small2[:, 0:LANES])
    gb_out_ref[...] = small2[:, LANES : 2 * LANES] * scale
    level_scale = level_sum / (count * radius * radius * radius)
    for i in range(ROWS):
        out_ref[:, i, :] = (din[i] - wet_slab(i) * level_scale)[0:LEVELS]

    forward(0)
    forward(1)

    def deliver(m, ref):
        drain(full.at[m, 1 - core], fwd_recv.at[m])
        for p in range(LEVELS // 8 + 1):
            rows = min(8, LEVELS - 8 * p)
            for c in range(2):
                ref[8 * p : 8 * p + rows, c * HALF : (c + 1) * HALF] = full[m, c, p, 0:rows, :]

    deliver(0, gw_out_ref)
    deliver(1, gw_in_ref)
    bias_tile, bias_row = LEVELS // 8, LEVELS % 8
    for c in range(2):
        gb_in_ref[:, c * HALF : (c + 1) * HALF] = full[1, c, bias_tile, bias_row : bias_row + 1, :]

    for copy in halo_copies + halo2_copies:
        copy.wait_send()
    for k, ref in enumerate((small_r1, small_r2, small2_r1, small2_r2)):
        drain(ref.at[pl.ds(0, ref.shape[0] - 1)], small_send.at[k])
    for m in range(2):
        drain(from_core.at[m], core_send.at[m])
        drain(from_plane.at[m, pl.ds(0, CHIPS - 1)], plane_send.at[m])
        drain(from_z.at[m, pl.ds(0, DEPTH - 1)], z_send.at[m])
        drain(full.at[m, core, pl.ds(0, CHIPS - 1)], gather_send.at[m])
        drain(full.at[m, core], fwd_send.at[m])


def store_results(out_v, gw_in_v, gb_in_v, gw_out_v, gb_out_v, out_h, gw_in_h, gb_in_ref, gw_out_h, gb_out_ref, sems):
    copies = []
    for n, (src, dst) in enumerate(((out_v, out_h), (gw_in_v, gw_in_h), (gw_out_v, gw_out_h))):
        copy = pltpu.make_async_copy(src, dst, sems.at[n])
        copy.start()
        copies.append(copy)
    gb_in_ref[...] = gb_in_v[...].reshape(HIDDEN)
    gb_out_ref[...] = gb_out_v[...].reshape(LANES)[0:LEVELS]
    for copy in copies:
        copy.wait()


def shards(tracer, cotangent, land_mask, bottom, kappa, w_in, b_in, w_out, b_out):
    vmem = pl.BlockSpec(memory_space=pltpu.VMEM)
    hbm = pl.BlockSpec(memory_space=pltpu.HBM)
    slab = (ROWS, PAD, LANES)
    levels = (LEVELS, ROWS, LANES)
    edge = (PAD, LANES)
    pieces = (CHIPS, 8, HALF)

    def v(*shape, dtype=F32):
        return pltpu.VMEM(shape, dtype)

    def sems(n):
        return pltpu.SemaphoreType.DMA((n,))

    scratch = [
        v(*levels), v(*levels), v(ROWS, LANES, dtype=jnp.int32), v(ROWS, LANES, dtype=jnp.int32),
        pltpu.SMEM((LEVELS,), F32), v(LEVELS, HIDDEN, dtype=BF16), v(HIDDEN),
        v(LEVELS, HIDDEN, dtype=BF16), pltpu.SMEM((LEVELS,), F32),
        v(*slab), v(*slab), v(*edge), v(*edge), v(*edge), v(*edge),
        v(4, *edge), v(4, *edge), v(4 * ROWS, LANES),
        v(1, LANES), v(PLANE, 1, LANES), v(1, LANES), v(DEPTH, 1, LANES),
        v(1, 2 * LANES), v(PLANE, 1, 2 * LANES), v(1, 2 * LANES), v(DEPTH, 1, 2 * LANES),
        v(LANES, HIDDEN), v(LANES, HIDDEN), v(LANES, HIDDEN, dtype=BF16),
        v(HIDDEN, LANES, dtype=BF16), v(LANES, HIDDEN, dtype=BF16), v(HIDDEN, LANES, dtype=BF16),
        v(LANES, COLS, dtype=BF16), v(HIDDEN, COLS, dtype=BF16), v(HIDDEN, COLS),
        v(HIDDEN, COLS, dtype=BF16), v(LANES, COLS, dtype=BF16), v(*slab),
        v(*levels), v(*levels), v(*levels), v(*levels), v(LEVELS + 1, ROWS, LANES),
        v(*levels), v(*levels), v(*levels), v(LANES, ROWS, LANES),
        v(2, 2, *pieces), v(2, *pieces), v(2, *pieces), v(2, *pieces), v(2, 8, HALF),
        v(2, DEPTH, 8, HALF), v(2, 8, HALF), v(2, 2, *pieces),
        sems(9), sems(4), sems(4), sems(2), sems(2), sems(2), sems(2),
        sems(2), sems(2), sems(2), sems(2), sems(2), sems(2), sems(8), sems(8),
    ]
    shapes = (
        jax.ShapeDtypeStruct(tracer.shape, F32),
        jax.ShapeDtypeStruct((LEVELS, HIDDEN), F32),
        jax.ShapeDtypeStruct((1, HIDDEN), F32),
        jax.ShapeDtypeStruct((LEVELS, HIDDEN), F32),
        jax.ShapeDtypeStruct((1, LANES), F32),
    )
    operands = (tracer, cotangent, land_mask, bottom, kappa, w_in, b_in, w_out.T, b_out)
    results = pl.pallas_call(
        kernel,
        out_shape=shapes,
        in_specs=[hbm] * 9,
        out_specs=(vmem,) * 5,
        scratch_shapes=scratch,
        compiler_params=pltpu.CompilerParams(
            collective_id=0, has_side_effects=True, vmem_limit_bytes=40 * 1024 * 1024
        ),
        name="step_adjoint",
    )(*(pltpu.with_memory_space_constraint(a, pltpu.HBM) for a in operands))
    out, gw_in, gb_in, gw_out, gb_out = pl.pallas_call(
        store_results,
        out_shape=shapes[:2]
        + (jax.ShapeDtypeStruct((HIDDEN,), F32), shapes[3], jax.ShapeDtypeStruct((LEVELS,), F32)),
        in_specs=[vmem] * 5,
        out_specs=(hbm, hbm, vmem, hbm, vmem),
        scratch_shapes=[sems(3)],
        compiler_params=pltpu.CompilerParams(vmem_limit_bytes=1024 * 1024),
        name="store_results",
    )(*results)
    return out, gw_in, gb_in, gw_out.T, gb_out


def solution(mesh):
    placed = (
        P(None, "lat", "lon"),
        P(None, "lat", "lon"),
        P("lat", "lon"),
        P("lat", "lon"),
        P(),
        P(),
        P(),
        P(),
        P(),
    )
    return jax.shard_map(
        shards,
        mesh=mesh,
        in_specs=placed,
        out_specs=(P(None, "lat", "lon"), P(), P(), P(), P()),
        check_vma=False,
    )
```

time: 55.3 us -> 45.4 us (0.82)
  local copies, waits for them, and re-layouts: 6.47 us -> 0 us
  Pallas kernels: 47.9 us -> 44.7 us
    unnamed x21 -> x0, local copies, waits for them, and re-layouts: 5.96 us -> none
    pallas_call x1 -> x2, Pallas kernels: 47.9 us -> 44.7 us  [the longest x1 43.2 us: shards(): pl.pallas_call(kernel, out_shape=shapes, in_specs=[hbm] * 9, out_specs=(v...]
where the time goes in v2:
time: 45.4 us; the launch traced here: 45.3 us
  Pallas kernels  44.7 us (98%)
  between operations  0.64 us (1%)
    pallas_call x1, Pallas kernels, shards(): pl.pallas_call(kernel, out_shape=shapes, in_specs=[hbm] * 9, out_specs=(v...  43.2 us
    pallas_call x1, Pallas kernels, shards(): pl.pallas_call(store_results, out_shape=shapes[:2] + (jax.ShapeDtypeStruc...  1.5 us

profile of v2, /device:TPU:1, one launch (start us, length us, event | category | flops | bytes accessed | tf_op | source)
XLA Modules:
  0.0 45.3 jit_solution(11935140156396671238)
XLA Ops:
  0.6 43.2 %step_adjoint.1 = (f32[100,8,128]{2,1,0:T(8,128)S(1)}, f32[100,512]{1,0:T(8,128)S(1)}, f32[1,512]{1,0:T(1,128)S(1)}, f32[100,512]{1,0:T(8,128)S(1)}, f32[1,128]{1,0:T(1,128)S(1)}) custom-call(f32[100,8,128]{2,1,0:T(8,128)} %tracer_hbm.1, f32[100,8,128]{2,1,0:T(8,128)} %cot_hbm.1, s32[8,128]{1,0:T(8,128)} %land_hbm.1, s32[8,128]{1,0:T(8,128)} %bottom_hbm.1, ...), custom_call_target="tpu_custom_call" | custom-call | tf_op jit(solution)/shard_map/step_adjoint/pallas_call | solution.py:527
  43.8 1.5 %store_results.1 = (f32[100,8,128]{2,1,0:T(8,128)}, f32[100,512]{1,0:T(8,128)}, f32[512]{0:T(512)}, f32[100,512]{1,0:T(8,128)}, f32[100]{0:T(128)}) custom-call(f32[100,8,128]{2,1,0:T(8,128)S(1)} %get-tuple-element.15.out_v, f32[100,512]{1,0:T(8,128)S(1)} %get-tuple-element.16.gw_in_v, f32[1,512]{1,0:T(1,128)S(1)} %get-tuple-element.17.gb_in_v, ...), custom_call_target="tpu_custom_call" | custom-call | tf_op jit(solution)/shard_map/store_results/pallas_call | solution.py:538

commit v3 on v2

--- a/solution.py
+++ b/solution.py
@@ -47,7 +47,7 @@
     tr_v, cot_v, land_v, bottom_v, kappa_s, w_in_v, b_in_v, w_out_v, b_out_s,
     slabs, adj_slabs, edge_hi, edge_lo, edge2_hi, edge2_lo, halo, halo2, near_depth,
     small_src, small_r1, small_mid, small_r2,
-    small2_src, small2_r1, small2_mid, small2_r2,
+    rows_src, rows_in,
     wi_f, wo_f, wi_b, w1t, wot, wo_b,
     inp, hid, slope, dpre, dlog, din,
     logit, mixed, val_x, val_y, mul_x, mul_y, gate, adj, dlev,
@@ -73,9 +73,9 @@
             (b_out_hbm, b_out_s),
         )
     ):
-        load = pltpu.make_async_copy(src, dst, load_sems.at[n])
+        loads.append(pltpu.make_async_copy(src, dst, load_sems.at[n]))
+    for load in loads[:3]:
         load.start()
-        loads.append(load)
 
     xs = [(x_me + d) % SIDE for d in range(SIDE)]
     ys = [(y_me + d) % SIDE for d in range(SIDE)]
@@ -97,11 +97,14 @@
     def greet(dev):
         pl.semaphore_signal(barrier, inc=1, device_id=dev, device_id_type=MESH)
 
+    greet(z_peer(Z_STEPS[0]))
     for step in everyone:
         greet(chip_peer(*step)[1])
-    for d in Z_STEPS:
+    for d in Z_STEPS[1:]:
         greet(z_peer(d))
     greet((lat, (lon + 2 * core - 1 + LON) % LON))
+    for load in loads[3:]:
+        load.start()
 
     row_id = lax.broadcasted_iota(jnp.int32, (PAD, LANES), 0)
     lane_id = lax.broadcasted_iota(jnp.int32, (PAD, LANES), 1)
@@ -118,20 +121,13 @@
         loads[n].wait()
     depth_all = (land_v[...] * bottom_v[...]).astype(F32)
     energy = jnp.zeros((PAD, LANES), F32)
-    hi = jnp.zeros((PAD, LANES), F32)
-    lo = jnp.zeros((PAD, LANES), F32)
     for i in range(ROWS):
         slabs[i, 0:LEVELS, :] = tr_v[:, i, :]
         slabs[i, LEVELS:PAD, :] = jnp.broadcast_to(depth_all[i : i + 1, :], (PAD - LEVELS, LANES))
-        x = slabs[i]
-        wet_x = jnp.where(row_f < depth_all[i : i + 1, :], x, 0.0)
+        wet_x = jnp.where(row_f < depth_all[i : i + 1, :], slabs[i], 0.0)
         energy = energy + wet_x * wet_x
-        hi = jnp.where(lane_id == i, pltpu.roll(x, i + 1, 1), hi)
-        lo = jnp.where(lane_id == i, pltpu.roll(x, i, 1) if i else x, lo)
     small_src[...] = as_row(jnp.sum(energy, axis=1, keepdims=True))
     small_r1[q_me] = small_src[...]
-    edge_hi[...] = hi
-    edge_lo[...] = lo
 
     pl.semaphore_wait(barrier, PLANE - 1 + DEPTH - 1 + 1)
 
@@ -139,10 +135,6 @@
         pltpu.make_async_remote_copy(
             src, dst, send, recv, device_id=dev, device_id_type=MESH
         ).start()
-
-    def small_plane(src, dst, which):
-        for step in everyone:
-            post(src, dst.at[q_me], chip_peer(*step)[1], small_send.at[which], small_recv.at[which])
 
     def send_z(src, dst, send, recv):
         for d in Z_STEPS:
@@ -167,7 +159,16 @@
             copies.append(copy)
         return copies
 
-    small_plane(small_src, small_r1, 0)
+    for step in everyone:
+        post(small_src, small_r1.at[q_me], chip_peer(*step)[1], small_send.at[0], small_recv.at[0])
+    hi = jnp.zeros((PAD, LANES), F32)
+    lo = jnp.zeros((PAD, LANES), F32)
+    for i in range(ROWS):
+        x = slabs[i]
+        hi = jnp.where(lane_id == i, pltpu.roll(x, i + 1, 1), hi)
+        lo = jnp.where(lane_id == i, pltpu.roll(x, i, 1) if i else x, lo)
+    edge_hi[...] = hi
+    edge_lo[...] = lo
     halo_copies = send_halo(0, (slabs.at[ROWS - 1], slabs.at[0], edge_hi, edge_lo), halo)
 
     for n in range(3, 6):
@@ -362,6 +363,9 @@
         lo = jnp.where(lane_l == i, pltpu.roll(x, i, 1) if i else x, lo)
     edge2_hi[0:LEVELS, :] = hi
     edge2_lo[0:LEVELS, :] = lo
+    halo2_copies = send_halo(
+        1, (adj_slabs.at[ROWS - 1], adj_slabs.at[0], edge2_hi, edge2_lo), halo2
+    )
 
     for j in range(COLS // width):
         cols = slice(j * width, (j + 1) * width)
@@ -369,15 +373,6 @@
         dpre[:, cols] = (back * slope[:, cols]).astype(BF16)
     share(1, lax.dot_general(inp[...], dpre[...], contract_last, preferred_element_type=F32))
 
-    def scatter(m):
-        drain(from_core.at[m], core_recv.at[m])
-        half[m] = grad[m, core] + from_core[m]
-        from_plane[m, p_me] = half[m, p_me]
-        for dx, dy in same_core:
-            p, dev = chip_peer(dx, dy, 0)
-            post(half.at[m, p], from_plane.at[m, p_me], dev, plane_send.at[m], plane_recv.at[m])
-
-    scatter(0)
     bout_row = lax.dot_general(
         jnp.ones((16, COLS), BF16), dlog[...], contract_last, preferred_element_type=F32
     )[0:1]
@@ -390,41 +385,22 @@
             part = out[0:PAD, s * LANES : (s + 1) * LANES]
             din[i] = part
             level = level + part * wet_slab(i)
-    small2_src[:, 0:LANES] = as_row(jnp.sum(level, axis=1, keepdims=True))
-    small2_src[:, LANES : 2 * LANES] = bout_row
-    small2_r1[q_me] = small2_src[...]
-    scatter(1)
-    small_plane(small2_src, small2_r1, 2)
-    halo2_copies = send_halo(
-        1, (adj_slabs.at[ROWS - 1], adj_slabs.at[0], edge2_hi, edge2_lo), halo2
-    )
-
-    def through_z(m):
-        drain(from_plane.at[m, pl.ds(0, CHIPS - 1)], plane_recv.at[m])
-        mid[m] = jnp.sum(from_plane[m], axis=0)
-        from_z[m, z_me] = mid[m]
-        send_z(mid.at[m], from_z.at[m], z_send.at[m], z_recv.at[m])
-
-    scale = 1.0 / math.sqrt(count)
-
-    def gather(m):
-        drain(from_z.at[m, pl.ds(0, DEPTH - 1)], z_recv.at[m])
-        chunk[m] = jnp.sum(from_z[m], axis=0) * scale
-        full[m, core, p_me] = chunk[m]
-        for dx, dy in same_core:
-            _, dev = chip_peer(dx, dy, 0)
-            post(chunk.at[m], full.at[m, core, p_me], dev, gather_send.at[m], gather_recv.at[m])
-
-    def forward(m):
-        drain(full.at[m, core, pl.ds(0, CHIPS - 1)], gather_recv.at[m])
-        post(full.at[m, core], full.at[m, core], partner, fwd_send.at[m], fwd_recv.at[m])
-
-    through_z(0)
-    through_z(1)
-    drain(small2_r1.at[pl.ds(0, PLANE - 1)], small_recv.at[2])
-    small2_mid[...] = jnp.sum(small2_r1[...], axis=0)
-    small2_r2[z_me] = small2_mid[...]
-    send_z(small2_mid, small2_r2, small_send.at[3], small_recv.at[3])
+    rows_src[:, 0:LANES] = as_row(jnp.sum(level, axis=1, keepdims=True))
+    rows_src[:, LANES : 2 * LANES] = bout_row
+    post(rows_src, rows_in, partner, core_send.at[2], core_recv.at[2])
+    for m in range(2):
+        drain(from_core.at[m], core_recv.at[m])
+        half[:, m] = grad[m, core] + from_core[m]
+    drain(rows_in, core_recv.at[2])
+    both_rows = rows_src[...] + rows_in[...]
+    tile, first = LEVELS // 8, LEVELS % 8
+    half[tile, 1, first + 1 : first + 2, 0:LANES] = both_rows[:, 0:LANES]
+    half[tile, 1, first + 2 : first + 3, 0:LANES] = both_rows[:, LANES : 2 * LANES]
+    from_plane[p_me] = half[p_me]
+    for dx, dy in same_core:
+        p, dev = chip_peer(dx, dy, 0)
+        post(half.at[p], from_plane.at[p_me], dev, plane_send.at[0], plane_recv.at[0])
+
     for copy in halo2_copies:
         copy.wait_recv()
     for i in range(ROWS):
@@ -432,43 +408,47 @@
         mix = flux(centre, near, i)
         wet = row_f < slabs[i, LEVELS : LEVELS + 1, :]
         din[i] = mix + jnp.where(wet, din[i] * inv_radius, 0.0)
-    gather(0)
-    gather(1)
-
-    drain(small2_r2.at[pl.ds(0, DEPTH - 1)], small_recv.at[3])
-    small2 = jnp.sum(small2_r2[...], axis=0)
-    level_sum = as_column(small2[:, 0:LANES])
-    gb_out_ref[...] = small2[:, LANES : 2 * LANES] * scale
+
+    drain(from_plane.at[pl.ds(0, CHIPS - 1)], plane_recv.at[0])
+    mid[...] = jnp.sum(from_plane[...], axis=0)
+    from_z[z_me] = mid[...]
+    send_z(mid, from_z, z_send.at[0], z_recv.at[0])
+    scale = 1.0 / math.sqrt(count)
+    drain(from_z.at[pl.ds(0, DEPTH - 1)], z_recv.at[0])
+    chunk[...] = jnp.sum(from_z[...], axis=0) * scale
+    full[core, p_me] = chunk[...]
+    for dx, dy in same_core:
+        _, dev = chip_peer(dx, dy, 0)
+        post(chunk, full.at[core, p_me], dev, gather_send.at[0], gather_recv.at[0])
+    drain(full.at[core, pl.ds(0, CHIPS - 1)], gather_recv.at[0])
+    post(full.at[core], full.at[core], partner, fwd_send.at[0], fwd_recv.at[0])
+
+    level_sum = as_column(full[core, tile, 1, first + 1 : first + 2, 0:LANES]) * math.sqrt(count)
+    gb_out_ref[...] = full[core, tile, 1, first + 2 : first + 3, 0:LANES]
     level_scale = level_sum / (count * radius * radius * radius)
     for i in range(ROWS):
         out_ref[:, i, :] = (din[i] - wet_slab(i) * level_scale)[0:LEVELS]
 
-    forward(0)
-    forward(1)
-
-    def deliver(m, ref):
-        drain(full.at[m, 1 - core], fwd_recv.at[m])
+    drain(full.at[1 - core], fwd_recv.at[0])
+    for m, ref in enumerate((gw_out_ref, gw_in_ref)):
         for p in range(LEVELS // 8 + 1):
             rows = min(8, LEVELS - 8 * p)
             for c in range(2):
-                ref[8 * p : 8 * p + rows, c * HALF : (c + 1) * HALF] = full[m, c, p, 0:rows, :]
-
-    deliver(0, gw_out_ref)
-    deliver(1, gw_in_ref)
-    bias_tile, bias_row = LEVELS // 8, LEVELS % 8
+                ref[8 * p : 8 * p + rows, c * HALF : (c + 1) * HALF] = full[c, p, m, 0:rows, :]
     for c in range(2):
-        gb_in_ref[:, c * HALF : (c + 1) * HALF] = full[1, c, bias_tile, bias_row : bias_row + 1, :]
+        gb_in_ref[:, c * HALF : (c + 1) * HALF] = full[c, tile, 1, first : first + 1, :]
 
     for copy in halo_copies + halo2_copies:
         copy.wait_send()
-    for k, ref in enumerate((small_r1, small_r2, small2_r1, small2_r2)):
-        drain(ref.at[pl.ds(0, ref.shape[0] - 1)], small_send.at[k])
+    drain(small_r1.at[pl.ds(0, PLANE - 1)], small_send.at[0])
+    drain(small_r2.at[pl.ds(0, DEPTH - 1)], small_send.at[1])
     for m in range(2):
         drain(from_core.at[m], core_send.at[m])
-        drain(from_plane.at[m, pl.ds(0, CHIPS - 1)], plane_send.at[m])
-        drain(from_z.at[m, pl.ds(0, DEPTH - 1)], z_send.at[m])
-        drain(full.at[m, core, pl.ds(0, CHIPS - 1)], gather_send.at[m])
-        drain(full.at[m, core], fwd_send.at[m])
+    drain(rows_in, core_send.at[2])
+    drain(from_plane.at[pl.ds(0, CHIPS - 1)], plane_send.at[0])
+    drain(from_z.at[pl.ds(0, DEPTH - 1)], z_send.at[0])
+    drain(full.at[core, pl.ds(0, CHIPS - 1)], gather_send.at[0])
+    drain(full.at[core], fwd_send.at[0])
 
 
 def store_results(out_v, gw_in_v, gb_in_v, gw_out_v, gb_out_v, out_h, gw_in_h, gb_in_ref, gw_out_h, gb_out_ref, sems):
@@ -490,6 +470,7 @@
     levels = (LEVELS, ROWS, LANES)
     edge = (PAD, LANES)
     pieces = (CHIPS, 8, HALF)
+    pair = (2, 8, HALF)
 
     def v(*shape, dtype=F32):
         return pltpu.VMEM(shape, dtype)
@@ -504,17 +485,17 @@
         v(*slab), v(*slab), v(*edge), v(*edge), v(*edge), v(*edge),
         v(4, *edge), v(4, *edge), v(4 * ROWS, LANES),
         v(1, LANES), v(PLANE, 1, LANES), v(1, LANES), v(DEPTH, 1, LANES),
-        v(1, 2 * LANES), v(PLANE, 1, 2 * LANES), v(1, 2 * LANES), v(DEPTH, 1, 2 * LANES),
+        v(1, 2 * LANES), v(1, 2 * LANES),
         v(LANES, HIDDEN), v(LANES, HIDDEN), v(LANES, HIDDEN, dtype=BF16),
         v(HIDDEN, LANES, dtype=BF16), v(LANES, HIDDEN, dtype=BF16), v(HIDDEN, LANES, dtype=BF16),
         v(LANES, COLS, dtype=BF16), v(HIDDEN, COLS, dtype=BF16), v(HIDDEN, COLS),
         v(HIDDEN, COLS, dtype=BF16), v(LANES, COLS, dtype=BF16), v(*slab),
         v(*levels), v(*levels), v(*levels), v(*levels), v(LEVELS + 1, ROWS, LANES),
         v(*levels), v(*levels), v(*levels), v(LANES, ROWS, LANES),
-        v(2, 2, *pieces), v(2, *pieces), v(2, *pieces), v(2, *pieces), v(2, 8, HALF),
-        v(2, DEPTH, 8, HALF), v(2, 8, HALF), v(2, 2, *pieces),
-        sems(9), sems(4), sems(4), sems(2), sems(2), sems(2), sems(2),
-        sems(2), sems(2), sems(2), sems(2), sems(2), sems(2), sems(8), sems(8),
+        v(2, 2, *pieces), v(2, *pieces), v(CHIPS, *pair), v(CHIPS, *pair), v(*pair),
+        v(DEPTH, *pair), v(*pair), v(2, CHIPS, *pair),
+        sems(9), sems(2), sems(2), sems(3), sems(3), sems(1), sems(1),
+        sems(1), sems(1), sems(1), sems(1), sems(1), sems(1), sems(8), sems(8),
     ]
     shapes = (
         jax.ShapeDtypeStruct(tracer.shape, F32),

time: 45.4 us -> 46.6 us (1.026)
  Pallas kernels: 44.7 us -> 45.9 us
    pallas_call x1, Pallas kernels: 43.2 us -> 44.4 us  [shards(): pl.pallas_call(kernel, out_shape=shapes, in_specs=[hbm] * 9, out_specs=(v...]
where the time goes in v3:
time: 46.6 us; the launch traced here: 46.5 us
  Pallas kernels  45.9 us (98%)
  between operations  0.64 us (1%)
    pallas_call x1, Pallas kernels, shards(): pl.pallas_call(kernel, out_shape=shapes, in_specs=[hbm] * 9, out_specs=(v...  44.4 us
    pallas_call x1, Pallas kernels, shards(): pl.pallas_call(store_results, out_shape=shapes[:2] + (jax.ShapeDtypeStruc...  1.5 us

profile of v3, /device:TPU:1, one launch (start us, length us, event | category | flops | bytes accessed | tf_op | source)
XLA Modules:
  0.0 46.5 jit_solution(2651524045425773886)
XLA Ops:
  0.6 44.4 %step_adjoint.1 = (f32[100,8,128]{2,1,0:T(8,128)S(1)}, f32[100,512]{1,0:T(8,128)S(1)}, f32[1,512]{1,0:T(1,128)S(1)}, f32[100,512]{1,0:T(8,128)S(1)}, f32[1,128]{1,0:T(1,128)S(1)}) custom-call(f32[100,8,128]{2,1,0:T(8,128)} %tracer_hbm.1, f32[100,8,128]{2,1,0:T(8,128)} %cot_hbm.1, s32[8,128]{1,0:T(8,128)} %land_hbm.1, s32[8,128]{1,0:T(8,128)} %bottom_hbm.1, ...), custom_call_target="tpu_custom_call" | custom-call | tf_op jit(solution)/shard_map/step_adjoint/pallas_call | solution.py:508
  45.0 1.5 %store_results.1 = (f32[100,8,128]{2,1,0:T(8,128)}, f32[100,512]{1,0:T(8,128)}, f32[512]{0:T(512)}, f32[100,512]{1,0:T(8,128)}, f32[100]{0:T(128)}) custom-call(f32[100,8,128]{2,1,0:T(8,128)S(1)} %get-tuple-element.15.out_v, f32[100,512]{1,0:T(8,128)S(1)} %get-tuple-element.16.gw_in_v, f32[1,512]{1,0:T(1,128)S(1)} %get-tuple-element.17.gb_in_v, ...), custom_call_target="tpu_custom_call" | custom-call | tf_op jit(solution)/shard_map/store_results/pallas_call | solution.py:519

commit v4 on v2

--- a/solution.py
+++ b/solution.py
@@ -47,7 +47,7 @@
     tr_v, cot_v, land_v, bottom_v, kappa_s, w_in_v, b_in_v, w_out_v, b_out_s,
     slabs, adj_slabs, edge_hi, edge_lo, edge2_hi, edge2_lo, halo, halo2, near_depth,
     small_src, small_r1, small_mid, small_r2,
-    small2_src, small2_r1, small2_mid, small2_r2,
+    rows_in,
     wi_f, wo_f, wi_b, w1t, wot, wo_b,
     inp, hid, slope, dpre, dlog, din,
     logit, mixed, val_x, val_y, mul_x, mul_y, gate, adj, dlev,
@@ -73,9 +73,9 @@
             (b_out_hbm, b_out_s),
         )
     ):
-        load = pltpu.make_async_copy(src, dst, load_sems.at[n])
+        loads.append(pltpu.make_async_copy(src, dst, load_sems.at[n]))
+    for load in loads[:3]:
         load.start()
-        loads.append(load)
 
     xs = [(x_me + d) % SIDE for d in range(SIDE)]
     ys = [(y_me + d) % SIDE for d in range(SIDE)]
@@ -97,11 +97,14 @@
     def greet(dev):
         pl.semaphore_signal(barrier, inc=1, device_id=dev, device_id_type=MESH)
 
+    greet(z_peer(Z_STEPS[0]))
     for step in everyone:
         greet(chip_peer(*step)[1])
-    for d in Z_STEPS:
+    for d in Z_STEPS[1:]:
         greet(z_peer(d))
     greet((lat, (lon + 2 * core - 1 + LON) % LON))
+    for load in loads[3:]:
+        load.start()
 
     row_id = lax.broadcasted_iota(jnp.int32, (PAD, LANES), 0)
     lane_id = lax.broadcasted_iota(jnp.int32, (PAD, LANES), 1)
@@ -118,20 +121,13 @@
         loads[n].wait()
     depth_all = (land_v[...] * bottom_v[...]).astype(F32)
     energy = jnp.zeros((PAD, LANES), F32)
-    hi = jnp.zeros((PAD, LANES), F32)
-    lo = jnp.zeros((PAD, LANES), F32)
     for i in range(ROWS):
         slabs[i, 0:LEVELS, :] = tr_v[:, i, :]
         slabs[i, LEVELS:PAD, :] = jnp.broadcast_to(depth_all[i : i + 1, :], (PAD - LEVELS, LANES))
-        x = slabs[i]
-        wet_x = jnp.where(row_f < depth_all[i : i + 1, :], x, 0.0)
+        wet_x = jnp.where(row_f < depth_all[i : i + 1, :], slabs[i], 0.0)
         energy = energy + wet_x * wet_x
-        hi = jnp.where(lane_id == i, pltpu.roll(x, i + 1, 1), hi)
-        lo = jnp.where(lane_id == i, pltpu.roll(x, i, 1) if i else x, lo)
     small_src[...] = as_row(jnp.sum(energy, axis=1, keepdims=True))
     small_r1[q_me] = small_src[...]
-    edge_hi[...] = hi
-    edge_lo[...] = lo
 
     pl.semaphore_wait(barrier, PLANE - 1 + DEPTH - 1 + 1)
 
@@ -139,10 +135,6 @@
         pltpu.make_async_remote_copy(
             src, dst, send, recv, device_id=dev, device_id_type=MESH
         ).start()
-
-    def small_plane(src, dst, which):
-        for step in everyone:
-            post(src, dst.at[q_me], chip_peer(*step)[1], small_send.at[which], small_recv.at[which])
 
     def send_z(src, dst, send, recv):
         for d in Z_STEPS:
@@ -167,7 +159,16 @@
             copies.append(copy)
         return copies
 
-    small_plane(small_src, small_r1, 0)
+    for step in everyone:
+        post(small_src, small_r1.at[q_me], chip_peer(*step)[1], small_send.at[0], small_recv.at[0])
+    hi = jnp.zeros((PAD, LANES), F32)
+    lo = jnp.zeros((PAD, LANES), F32)
+    for i in range(ROWS):
+        x = slabs[i]
+        hi = jnp.where(lane_id == i, pltpu.roll(x, i + 1, 1), hi)
+        lo = jnp.where(lane_id == i, pltpu.roll(x, i, 1) if i else x, lo)
+    edge_hi[...] = hi
+    edge_lo[...] = lo
     halo_copies = send_halo(0, (slabs.at[ROWS - 1], slabs.at[0], edge_hi, edge_lo), halo)
 
     for n in range(3, 6):
@@ -352,17 +353,6 @@
 
     share(0, lax.dot_general(dlog[...], hid[...], contract_last, preferred_element_type=F32))
 
-    hi = jnp.zeros((LEVELS, LANES), F32)
-    lo = jnp.zeros((LEVELS, LANES), F32)
-    lane_l = lane_id[0:LEVELS]
-    for i in range(ROWS):
-        x = adj[:, i, :]
-        adj_slabs[i, 0:LEVELS, :] = x
-        hi = jnp.where(lane_l == i, pltpu.roll(x, i + 1, 1), hi)
-        lo = jnp.where(lane_l == i, pltpu.roll(x, i, 1) if i else x, lo)
-    edge2_hi[0:LEVELS, :] = hi
-    edge2_lo[0:LEVELS, :] = lo
-
     for j in range(COLS // width):
         cols = slice(j * width, (j + 1) * width)
         back = jnp.dot(wo_b[...], dlog[:, cols], preferred_element_type=F32)
@@ -370,13 +360,14 @@
     share(1, lax.dot_general(inp[...], dpre[...], contract_last, preferred_element_type=F32))
 
     def scatter(m):
-        drain(from_core.at[m], core_recv.at[m])
-        half[m] = grad[m, core] + from_core[m]
-        from_plane[m, p_me] = half[m, p_me]
         for dx, dy in same_core:
             p, dev = chip_peer(dx, dy, 0)
             post(half.at[m, p], from_plane.at[m, p_me], dev, plane_send.at[m], plane_recv.at[m])
 
+    tile, first = LEVELS // 8, LEVELS % 8
+    drain(from_core.at[0], core_recv.at[0])
+    half[0] = grad[0, core] + from_core[0]
+    from_plane[0, p_me] = half[0, p_me]
     scatter(0)
     bout_row = lax.dot_general(
         jnp.ones((16, COLS), BF16), dlog[...], contract_last, preferred_element_type=F32
@@ -390,14 +381,24 @@
             part = out[0:PAD, s * LANES : (s + 1) * LANES]
             din[i] = part
             level = level + part * wet_slab(i)
-    small2_src[:, 0:LANES] = as_row(jnp.sum(level, axis=1, keepdims=True))
-    small2_src[:, LANES : 2 * LANES] = bout_row
-    small2_r1[q_me] = small2_src[...]
+    level_row = as_row(jnp.sum(level, axis=1, keepdims=True))
+    drain(from_core.at[1], core_recv.at[1])
+    half[1] = grad[1, core] + from_core[1]
+    half[1, tile, first + 1 : first + 2, 0:LANES] = level_row
+    half[1, tile, first + 2 : first + 3, 0:LANES] = bout_row
+    from_plane[1, p_me] = half[1, p_me]
     scatter(1)
-    small_plane(small2_src, small2_r1, 2)
-    halo2_copies = send_halo(
-        1, (adj_slabs.at[ROWS - 1], adj_slabs.at[0], edge2_hi, edge2_lo), halo2
-    )
+
+    hi = jnp.zeros((LEVELS, LANES), F32)
+    lo = jnp.zeros((LEVELS, LANES), F32)
+    lane_l = lane_id[0:LEVELS]
+    for i in range(ROWS):
+        x = adj[:, i, :]
+        adj_slabs[i, 0:LEVELS, :] = x
+        hi = jnp.where(lane_l == i, pltpu.roll(x, i + 1, 1), hi)
+        lo = jnp.where(lane_l == i, pltpu.roll(x, i, 1) if i else x, lo)
+    edge2_hi[0:LEVELS, :] = hi
+    edge2_lo[0:LEVELS, :] = lo
 
     def through_z(m):
         drain(from_plane.at[m, pl.ds(0, CHIPS - 1)], plane_recv.at[m])
@@ -415,16 +416,14 @@
             _, dev = chip_peer(dx, dy, 0)
             post(chunk.at[m], full.at[m, core, p_me], dev, gather_send.at[m], gather_recv.at[m])
 
-    def forward(m):
-        drain(full.at[m, core, pl.ds(0, CHIPS - 1)], gather_recv.at[m])
-        post(full.at[m, core], full.at[m, core], partner, fwd_send.at[m], fwd_recv.at[m])
-
     through_z(0)
     through_z(1)
-    drain(small2_r1.at[pl.ds(0, PLANE - 1)], small_recv.at[2])
-    small2_mid[...] = jnp.sum(small2_r1[...], axis=0)
-    small2_r2[z_me] = small2_mid[...]
-    send_z(small2_mid, small2_r2, small_send.at[3], small_recv.at[3])
+    halo2_copies = send_halo(
+        1, (adj_slabs.at[ROWS - 1], adj_slabs.at[0], edge2_hi, edge2_lo), halo2
+    )
+    gather(0)
+    gather(1)
+
     for copy in halo2_copies:
         copy.wait_recv()
     for i in range(ROWS):
@@ -432,19 +431,12 @@
         mix = flux(centre, near, i)
         wet = row_f < slabs[i, LEVELS : LEVELS + 1, :]
         din[i] = mix + jnp.where(wet, din[i] * inv_radius, 0.0)
-    gather(0)
-    gather(1)
-
-    drain(small2_r2.at[pl.ds(0, DEPTH - 1)], small_recv.at[3])
-    small2 = jnp.sum(small2_r2[...], axis=0)
-    level_sum = as_column(small2[:, 0:LANES])
-    gb_out_ref[...] = small2[:, LANES : 2 * LANES] * scale
-    level_scale = level_sum / (count * radius * radius * radius)
-    for i in range(ROWS):
-        out_ref[:, i, :] = (din[i] - wet_slab(i) * level_scale)[0:LEVELS]
-
-    forward(0)
-    forward(1)
+
+    def forward(m):
+        drain(full.at[m, core, pl.ds(0, CHIPS - 1)], gather_recv.at[m])
+        if m:
+            post(full.at[m, core, tile], rows_in, partner, core_send.at[2], core_recv.at[2])
+        post(full.at[m, core], full.at[m, core], partner, fwd_send.at[m], fwd_recv.at[m])
 
     def deliver(m, ref):
         drain(full.at[m, 1 - core], fwd_recv.at[m])
@@ -453,22 +445,31 @@
             for c in range(2):
                 ref[8 * p : 8 * p + rows, c * HALF : (c + 1) * HALF] = full[m, c, p, 0:rows, :]
 
+    forward(0)
+    forward(1)
     deliver(0, gw_out_ref)
+    drain(rows_in, core_recv.at[2])
+    both_rows = full[1, core, tile, first + 1 : first + 3, 0:LANES] + rows_in[first + 1 : first + 3, 0:LANES]
+    level_sum = as_column(both_rows[0:1]) * math.sqrt(count)
+    gb_out_ref[...] = both_rows[1:2]
+    level_scale = level_sum / (count * radius * radius * radius)
+    for i in range(ROWS):
+        out_ref[:, i, :] = (din[i] - wet_slab(i) * level_scale)[0:LEVELS]
     deliver(1, gw_in_ref)
-    bias_tile, bias_row = LEVELS // 8, LEVELS % 8
     for c in range(2):
-        gb_in_ref[:, c * HALF : (c + 1) * HALF] = full[1, c, bias_tile, bias_row : bias_row + 1, :]
+        gb_in_ref[:, c * HALF : (c + 1) * HALF] = full[1, c, tile, first : first + 1, :]
 
     for copy in halo_copies + halo2_copies:
         copy.wait_send()
-    for k, ref in enumerate((small_r1, small_r2, small2_r1, small2_r2)):
-        drain(ref.at[pl.ds(0, ref.shape[0] - 1)], small_send.at[k])
+    drain(small_r1.at[pl.ds(0, PLANE - 1)], small_send.at[0])
+    drain(small_r2.at[pl.ds(0, DEPTH - 1)], small_send.at[1])
     for m in range(2):
         drain(from_core.at[m], core_send.at[m])
         drain(from_plane.at[m, pl.ds(0, CHIPS - 1)], plane_send.at[m])
         drain(from_z.at[m, pl.ds(0, DEPTH - 1)], z_send.at[m])
         drain(full.at[m, core, pl.ds(0, CHIPS - 1)], gather_send.at[m])
         drain(full.at[m, core], fwd_send.at[m])
+    drain(rows_in, core_send.at[2])
 
 
 def store_results(out_v, gw_in_v, gb_in_v, gw_out_v, gb_out_v, out_h, gw_in_h, gb_in_ref, gw_out_h, gb_out_ref, sems):
@@ -504,7 +505,7 @@
         v(*slab), v(*slab), v(*edge), v(*edge), v(*edge), v(*edge),
         v(4, *edge), v(4, *edge), v(4 * ROWS, LANES),
         v(1, LANES), v(PLANE, 1, LANES), v(1, LANES), v(DEPTH, 1, LANES),
-        v(1, 2 * LANES), v(PLANE, 1, 2 * LANES), v(1, 2 * LANES), v(DEPTH, 1, 2 * LANES),
+        v(8, HALF),
         v(LANES, HIDDEN), v(LANES, HIDDEN), v(LANES, HIDDEN, dtype=BF16),
         v(HIDDEN, LANES, dtype=BF16), v(LANES, HIDDEN, dtype=BF16), v(HIDDEN, LANES, dtype=BF16),
         v(LANES, COLS, dtype=BF16), v(HIDDEN, COLS, dtype=BF16), v(HIDDEN, COLS),
@@ -513,7 +514,7 @@
         v(*levels), v(*levels), v(*levels), v(LANES, ROWS, LANES),
         v(2, 2, *pieces), v(2, *pieces), v(2, *pieces), v(2, *pieces), v(2, 8, HALF),
         v(2, DEPTH, 8, HALF), v(2, 8, HALF), v(2, 2, *pieces),
-        sems(9), sems(4), sems(4), sems(2), sems(2), sems(2), sems(2),
+        sems(9), sems(2), sems(2), sems(3), sems(3), sems(2), sems(2),
         sems(2), sems(2), sems(2), sems(2), sems(2), sems(2), sems(8), sems(8),
     ]
     shapes = (

time: 45.4 us -> 45 us (level)
  no operation moved by 1% of the time
where the time goes in v4:
time: 45 us; the launch traced here: 44.9 us
  Pallas kernels  44.3 us (98%)
  between operations  0.64 us (1%)
    pallas_call x1, Pallas kernels, shards(): pl.pallas_call(kernel, out_shape=shapes, in_specs=[hbm] * 9, out_specs=(v...  42.8 us
    pallas_call x1, Pallas kernels, shards(): pl.pallas_call(store_results, out_shape=shapes[:2] + (jax.ShapeDtypeStruc...  1.5 us

profile of v4, /device:TPU:1, one launch (start us, length us, event | category | flops | bytes accessed | tf_op | source)
XLA Modules:
  0.0 44.9 jit_solution(11507139190628119581)
XLA Ops:
  0.6 42.8 %step_adjoint.1 = (f32[100,8,128]{2,1,0:T(8,128)S(1)}, f32[100,512]{1,0:T(8,128)S(1)}, f32[1,512]{1,0:T(1,128)S(1)}, f32[100,512]{1,0:T(8,128)S(1)}, f32[1,128]{1,0:T(1,128)S(1)}) custom-call(f32[100,8,128]{2,1,0:T(8,128)} %tracer_hbm.1, f32[100,8,128]{2,1,0:T(8,128)} %cot_hbm.1, s32[8,128]{1,0:T(8,128)} %land_hbm.1, s32[8,128]{1,0:T(8,128)} %bottom_hbm.1, ...), custom_call_target="tpu_custom_call" | custom-call | tf_op jit(solution)/shard_map/step_adjoint/pallas_call | solution.py:528
  43.4 1.5 %store_results.1 = (f32[100,8,128]{2,1,0:T(8,128)}, f32[100,512]{1,0:T(8,128)}, f32[512]{0:T(512)}, f32[100,512]{1,0:T(8,128)}, f32[100]{0:T(128)}) custom-call(f32[100,8,128]{2,1,0:T(8,128)S(1)} %get-tuple-element.15.out_v, f32[100,512]{1,0:T(8,128)S(1)} %get-tuple-element.16.gw_in_v, f32[1,512]{1,0:T(1,128)S(1)} %get-tuple-element.17.gb_in_v, ...), custom_call_target="tpu_custom_call" | custom-call | tf_op jit(solution)/shard_map/store_results/pallas_call | solution.py:539

commit v5 on v4

--- a/solution.py
+++ b/solution.py
@@ -28,6 +28,7 @@
 PLANE = 2 * CHIPS
 DEPTH = 8
 HALF = HIDDEN // 2
+REDUCERS = PAD // 8
 
 
 def ring(d, n):
@@ -47,11 +48,10 @@
     tr_v, cot_v, land_v, bottom_v, kappa_s, w_in_v, b_in_v, w_out_v, b_out_s,
     slabs, adj_slabs, edge_hi, edge_lo, edge2_hi, edge2_lo, halo, halo2, near_depth,
     small_src, small_r1, small_mid, small_r2,
-    rows_in,
-    wi_f, wo_f, wi_b, w1t, wot, wo_b,
+    wi_f, wi_half, wo_f, wi_b, w1t, wot, wo_b,
     inp, hid, slope, dpre, dlog, din,
     logit, mixed, val_x, val_y, mul_x, mul_y, gate, adj, dlev,
-    grad, from_core, half, from_plane, mid, from_z, chunk, full,
+    given, kept, from_core, half, from_plane, mid, from_z, chunk, full,
     load_sems, small_send, small_recv, core_send, core_recv, plane_send, plane_recv,
     z_send, z_recv, gather_send, gather_recv, fwd_send, fwd_recv, halo_send, halo_recv,
 ):
@@ -63,6 +63,8 @@
     core = lon % 2
     p_me = x_me * SIDE + y_me
     q_me = p_me * 2 + core
+    reducer = p_me < REDUCERS
+    idle = p_me >= REDUCERS
     lon_z = z_me * 2
 
     loads = []
@@ -183,6 +185,8 @@
     wi_f[LEVELS + 1 : LEVELS + 2, :] = bias_mid
     wi_f[LEVELS + 2 : LEVELS + 3, :] = bias_lo
     wi_b[...] = wi_f[...].astype(BF16)
+    for c in range(2):
+        wi_half[c] = wi_f[0:PAD, c * HALF : (c + 1) * HALF]
     w1t[...] = wi_f[...].T.astype(BF16)
     wo_f[LEVELS:LANES, :] = jnp.zeros((LANES - LEVELS, HIDDEN), F32)
     wo_f[0:LEVELS, :] = w_out_v[...].astype(F32)
@@ -343,51 +347,40 @@
 
     for i in range(ROWS):
         dlog[:, i * LANES : (i + 1) * LANES] = dlev[:, i, :].astype(BF16)
-    contract_last = (((1,), (1,)), ((), ()))
-
-    def share(m, value):
-        for p in range(CHIPS):
-            for c in range(2):
-                grad[m, c, p] = value[8 * p : 8 * p + 8, c * HALF : (c + 1) * HALF]
-        post(grad.at[m, 1 - core], from_core.at[m], partner, core_send.at[m], core_recv.at[m])
-
-    share(0, lax.dot_general(dlog[...], hid[...], contract_last, preferred_element_type=F32))
-
     for j in range(COLS // width):
         cols = slice(j * width, (j + 1) * width)
         back = jnp.dot(wo_b[...], dlog[:, cols], preferred_element_type=F32)
         dpre[:, cols] = (back * slope[:, cols]).astype(BF16)
-    share(1, lax.dot_general(inp[...], dpre[...], contract_last, preferred_element_type=F32))
-
-    def scatter(m):
-        for dx, dy in same_core:
-            p, dev = chip_peer(dx, dy, 0)
-            post(half.at[m, p], from_plane.at[m, p_me], dev, plane_send.at[m], plane_recv.at[m])
-
-    tile, first = LEVELS // 8, LEVELS % 8
-    drain(from_core.at[0], core_recv.at[0])
-    half[0] = grad[0, core] + from_core[0]
-    from_plane[0, p_me] = half[0, p_me]
-    scatter(0)
+    contract_last = (((1,), (1,)), ((), ()))
+    sources = ((inp, dpre), (dlog, hid))
+
+    def half_of(m, c):
+        small, big = sources[m]
+        rows = big[pl.ds(pl.multiple_of(c * HALF, HALF), HALF), :]
+        value = lax.dot_general(small[...], rows, contract_last, preferred_element_type=F32)
+        return value[0:PAD].reshape(REDUCERS, 8, HALF)
+
+    for m in range(2):
+        given[m] = half_of(m, 1 - core)
+        post(given.at[m], from_core.at[m], partner, core_send.at[m], core_recv.at[m])
+    for m in range(2):
+        kept[m] = half_of(m, core)
     bout_row = lax.dot_general(
         jnp.ones((16, COLS), BF16), dlog[...], contract_last, preferred_element_type=F32
     )[0:1]
-    level = jnp.zeros((PAD, LANES), F32)
-    for j in range(COLS // width):
-        cols = slice(j * width, (j + 1) * width)
-        out = jnp.dot(wi_b[...], dpre[:, cols], preferred_element_type=F32)
-        for s in range(width // LANES):
-            i = j * (width // LANES) + s
-            part = out[0:PAD, s * LANES : (s + 1) * LANES]
-            din[i] = part
-            level = level + part * wet_slab(i)
-    level_row = as_row(jnp.sum(level, axis=1, keepdims=True))
-    drain(from_core.at[1], core_recv.at[1])
-    half[1] = grad[1, core] + from_core[1]
-    half[1, tile, first + 1 : first + 2, 0:LANES] = level_row
-    half[1, tile, first + 2 : first + 3, 0:LANES] = bout_row
-    from_plane[1, p_me] = half[1, p_me]
-    scatter(1)
+    tile, first = LEVELS // 8, LEVELS % 8
+
+    for m in range(2):
+        drain(from_core.at[m], core_recv.at[m])
+        half[m] = kept[m] + from_core[m]
+        if m:
+            half[1, tile, first : first + 1, 0:LANES] = bout_row
+        for dx, dy in same_core:
+            p, dev = chip_peer(dx, dy, 0)
+
+            @pl.when(p < REDUCERS)
+            def _(m=m, p=p, dev=dev):
+                post(half.at[m, p], from_plane.at[m, p_me], dev, plane_send.at[m], plane_recv.at[m])
 
     hi = jnp.zeros((LEVELS, LANES), F32)
     lo = jnp.zeros((LEVELS, LANES), F32)
@@ -399,65 +392,80 @@
         lo = jnp.where(lane_l == i, pltpu.roll(x, i, 1) if i else x, lo)
     edge2_hi[0:LEVELS, :] = hi
     edge2_lo[0:LEVELS, :] = lo
-
-    def through_z(m):
-        drain(from_plane.at[m, pl.ds(0, CHIPS - 1)], plane_recv.at[m])
-        mid[m] = jnp.sum(from_plane[m], axis=0)
-        from_z[m, z_me] = mid[m]
-        send_z(mid.at[m], from_z.at[m], z_send.at[m], z_recv.at[m])
+    for j in range(COLS // width):
+        cols = slice(j * width, (j + 1) * width)
+        out = jnp.dot(wi_b[...], dpre[:, cols], preferred_element_type=F32)
+        for s in range(width // LANES):
+            i = j * (width // LANES) + s
+            din[i] = out[0:PAD, s * LANES : (s + 1) * LANES] * inv_radius
 
     scale = 1.0 / math.sqrt(count)
-
-    def gather(m):
-        drain(from_z.at[m, pl.ds(0, DEPTH - 1)], z_recv.at[m])
-        chunk[m] = jnp.sum(from_z[m], axis=0) * scale
-        full[m, core, p_me] = chunk[m]
-        for dx, dy in same_core:
-            _, dev = chip_peer(dx, dy, 0)
-            post(chunk.at[m], full.at[m, core, p_me], dev, gather_send.at[m], gather_recv.at[m])
-
-    through_z(0)
-    through_z(1)
+    for m in range(2):
+
+        @pl.when(reducer)
+        def _(m=m):
+            from_plane[m, p_me] = half[m, p_me]
+            drain(from_plane.at[m, pl.ds(0, CHIPS - 1)], plane_recv.at[m])
+            mid[m] = jnp.sum(from_plane[m], axis=0)
+            from_z[m, z_me] = mid[m]
+            send_z(mid.at[m], from_z.at[m], z_send.at[m], z_recv.at[m])
+
     halo2_copies = send_halo(
         1, (adj_slabs.at[ROWS - 1], adj_slabs.at[0], edge2_hi, edge2_lo), halo2
     )
-    gather(0)
-    gather(1)
+    for m in range(2):
+
+        @pl.when(reducer)
+        def _(m=m):
+            drain(from_z.at[m, pl.ds(0, DEPTH - 1)], z_recv.at[m])
+            chunk[m] = jnp.sum(from_z[m], axis=0) * scale
+            full[m, core, p_me] = chunk[m]
+            for dx, dy in same_core:
+                _, dev = chip_peer(dx, dy, 0)
+                post(chunk.at[m], full.at[m, core, p_me], dev, gather_send.at[m], gather_recv.at[m])
 
     for copy in halo2_copies:
         copy.wait_recv()
     for i in range(ROWS):
         centre, near = neighbours(adj_slabs, halo2, i)
-        mix = flux(centre, near, i)
         wet = row_f < slabs[i, LEVELS : LEVELS + 1, :]
-        din[i] = mix + jnp.where(wet, din[i] * inv_radius, 0.0)
-
-    def forward(m):
-        drain(full.at[m, core, pl.ds(0, CHIPS - 1)], gather_recv.at[m])
-        if m:
-            post(full.at[m, core, tile], rows_in, partner, core_send.at[2], core_recv.at[2])
+        din[i] = flux(centre, near, i) + jnp.where(wet, din[i], 0.0)
+
+    def drain_peers(ref, sem):
+        @pl.when(reducer)
+        def _():
+            drain(ref.at[pl.ds(0, REDUCERS - 1)], sem)
+
+        @pl.when(idle)
+        def _():
+            drain(ref, sem)
+
+    for m in range(2):
+        drain_peers(full.at[m, core], gather_recv.at[m])
         post(full.at[m, core], full.at[m, core], partner, fwd_send.at[m], fwd_recv.at[m])
 
     def deliver(m, ref):
-        drain(full.at[m, 1 - core], fwd_recv.at[m])
-        for p in range(LEVELS // 8 + 1):
+        for p in range(REDUCERS):
             rows = min(8, LEVELS - 8 * p)
             for c in range(2):
                 ref[8 * p : 8 * p + rows, c * HALF : (c + 1) * HALF] = full[m, c, p, 0:rows, :]
 
-    forward(0)
-    forward(1)
-    deliver(0, gw_out_ref)
-    drain(rows_in, core_recv.at[2])
-    both_rows = full[1, core, tile, first + 1 : first + 3, 0:LANES] + rows_in[first + 1 : first + 3, 0:LANES]
-    level_sum = as_column(both_rows[0:1]) * math.sqrt(count)
-    gb_out_ref[...] = both_rows[1:2]
+    drain(full.at[0, 1 - core], fwd_recv.at[0])
+    weighted = jnp.zeros((PAD, HALF), F32)
+    for c in range(2):
+        weighted = weighted + wi_half[c] * full[0, c].reshape(PAD, HALF)
+    level_sum = radius * jnp.sum(weighted, axis=1, keepdims=True) * math.sqrt(count)
     level_scale = level_sum / (count * radius * radius * radius)
     for i in range(ROWS):
         out_ref[:, i, :] = (din[i] - wet_slab(i) * level_scale)[0:LEVELS]
-    deliver(1, gw_in_ref)
+    deliver(0, gw_in_ref)
     for c in range(2):
-        gb_in_ref[:, c * HALF : (c + 1) * HALF] = full[1, c, tile, first : first + 1, :]
+        gb_in_ref[:, c * HALF : (c + 1) * HALF] = full[0, c, tile, first : first + 1, :]
+    drain(full.at[1, 1 - core], fwd_recv.at[1])
+    deliver(1, gw_out_ref)
+    gb_out_ref[...] = (
+        full[1, 0, tile, first : first + 1, 0:LANES] + full[1, 1, tile, first : first + 1, 0:LANES]
+    )
 
     for copy in halo_copies + halo2_copies:
         copy.wait_send()
@@ -465,11 +473,14 @@
     drain(small_r2.at[pl.ds(0, DEPTH - 1)], small_send.at[1])
     for m in range(2):
         drain(from_core.at[m], core_send.at[m])
-        drain(from_plane.at[m, pl.ds(0, CHIPS - 1)], plane_send.at[m])
-        drain(from_z.at[m, pl.ds(0, DEPTH - 1)], z_send.at[m])
-        drain(full.at[m, core, pl.ds(0, CHIPS - 1)], gather_send.at[m])
+        drain_peers(half.at[m], plane_send.at[m])
+
+        @pl.when(reducer)
+        def _(m=m):
+            drain(from_z.at[m, pl.ds(0, DEPTH - 1)], z_send.at[m])
+            drain(from_plane.at[m, pl.ds(0, CHIPS - 1)], gather_send.at[m])
+
         drain(full.at[m, core], fwd_send.at[m])
-    drain(rows_in, core_send.at[2])
 
 
 def store_results(out_v, gw_in_v, gb_in_v, gw_out_v, gb_out_v, out_h, gw_in_h, gb_in_ref, gw_out_h, gb_out_ref, sems):
@@ -490,7 +501,7 @@
     slab = (ROWS, PAD, LANES)
     levels = (LEVELS, ROWS, LANES)
     edge = (PAD, LANES)
-    pieces = (CHIPS, 8, HALF)
+    pieces = (REDUCERS, 8, HALF)
 
     def v(*shape, dtype=F32):
         return pltpu.VMEM(shape, dtype)
@@ -505,16 +516,15 @@
         v(*slab), v(*slab), v(*edge), v(*edge), v(*edge), v(*edge),
         v(4, *edge), v(4, *edge), v(4 * ROWS, LANES),
         v(1, LANES), v(PLANE, 1, LANES), v(1, LANES), v(DEPTH, 1, LANES),
-        v(8, HALF),
-        v(LANES, HIDDEN), v(LANES, HIDDEN), v(LANES, HIDDEN, dtype=BF16),
+        v(LANES, HIDDEN), v(2, PAD, HALF), v(LANES, HIDDEN), v(LANES, HIDDEN, dtype=BF16),
         v(HIDDEN, LANES, dtype=BF16), v(LANES, HIDDEN, dtype=BF16), v(HIDDEN, LANES, dtype=BF16),
         v(LANES, COLS, dtype=BF16), v(HIDDEN, COLS, dtype=BF16), v(HIDDEN, COLS),
         v(HIDDEN, COLS, dtype=BF16), v(LANES, COLS, dtype=BF16), v(*slab),
         v(*levels), v(*levels), v(*levels), v(*levels), v(LEVELS + 1, ROWS, LANES),
         v(*levels), v(*levels), v(*levels), v(LANES, ROWS, LANES),
-        v(2, 2, *pieces), v(2, *pieces), v(2, *pieces), v(2, *pieces), v(2, 8, HALF),
-        v(2, DEPTH, 8, HALF), v(2, 8, HALF), v(2, 2, *pieces),
-        sems(9), sems(2), sems(2), sems(3), sems(3), sems(2), sems(2),
+        v(2, *pieces), v(2, *pieces), v(2, *pieces), v(2, *pieces), v(2, CHIPS, 8, HALF),
+        v(2, 8, HALF), v(2, DEPTH, 8, HALF), v(2, 8, HALF), v(2, 2, *pieces),
+        sems(9), sems(2), sems(2), sems(2), sems(2), sems(2), sems(2),
         sems(2), sems(2), sems(2), sems(2), sems(2), sems(2), sems(8), sems(8),
     ]
     shapes = (

time: 45 us -> 45.2 us (level)
  no operation moved by 1% of the time
where the time goes in v5:
time: 45.2 us; the launch traced here: 45.1 us
  Pallas kernels  44.5 us (98%)
  between operations  0.64 us (1%)
    pallas_call x1, Pallas kernels, shards(): pl.pallas_call(kernel, out_shape=shapes, in_specs=[hbm] * 9, out_specs=(v...  43 us
    pallas_call x1, Pallas kernels, shards(): pl.pallas_call(store_results, out_shape=shapes[:2] + (jax.ShapeDtypeStruc...  1.5 us

profile of v5, /device:TPU:1, one launch (start us, length us, event | category | flops | bytes accessed | tf_op | source)
XLA Modules:
  0.0 45.1 jit_solution(14491023271802308783)
XLA Ops:
  0.6 43.0 %step_adjoint.1 = (f32[100,8,128]{2,1,0:T(8,128)S(1)}, f32[100,512]{1,0:T(8,128)S(1)}, f32[1,512]{1,0:T(1,128)S(1)}, f32[100,512]{1,0:T(8,128)S(1)}, f32[1,128]{1,0:T(1,128)S(1)}) custom-call(f32[100,8,128]{2,1,0:T(8,128)} %tracer_hbm.1, f32[100,8,128]{2,1,0:T(8,128)} %cot_hbm.1, s32[8,128]{1,0:T(8,128)} %land_hbm.1, s32[8,128]{1,0:T(8,128)} %bottom_hbm.1, ...), custom_call_target="tpu_custom_call" | custom-call | tf_op jit(solution)/shard_map/step_adjoint/pallas_call | solution.py:538
  43.6 1.5 %store_results.1 = (f32[100,8,128]{2,1,0:T(8,128)}, f32[100,512]{1,0:T(8,128)}, f32[512]{0:T(512)}, f32[100,512]{1,0:T(8,128)}, f32[100]{0:T(128)}) custom-call(f32[100,8,128]{2,1,0:T(8,128)S(1)} %get-tuple-element.15.out_v, f32[100,512]{1,0:T(8,128)S(1)} %get-tuple-element.16.gw_in_v, f32[1,512]{1,0:T(1,128)S(1)} %get-tuple-element.17.gb_in_v, ...), custom_call_target="tpu_custom_call" | custom-call | tf_op jit(solution)/shard_map/store_results/pallas_call | solution.py:549

commit v6 on v5

--- a/solution.py
+++ b/solution.py
@@ -28,7 +28,7 @@
 PLANE = 2 * CHIPS
 DEPTH = 8
 HALF = HIDDEN // 2
-REDUCERS = PAD // 8
+ROWS_EACH = 2 * PAD // CHIPS
 
 
 def ring(d, n):
@@ -48,7 +48,7 @@
     tr_v, cot_v, land_v, bottom_v, kappa_s, w_in_v, b_in_v, w_out_v, b_out_s,
     slabs, adj_slabs, edge_hi, edge_lo, edge2_hi, edge2_lo, halo, halo2, near_depth,
     small_src, small_r1, small_mid, small_r2,
-    wi_f, wi_half, wo_f, wi_b, w1t, wot, wo_b,
+    wi_f, wo_f, wi_b, w1t, wot, wo_b,
     inp, hid, slope, dpre, dlog, din,
     logit, mixed, val_x, val_y, mul_x, mul_y, gate, adj, dlev,
     given, kept, from_core, half, from_plane, mid, from_z, chunk, full,
@@ -63,8 +63,7 @@
     core = lon % 2
     p_me = x_me * SIDE + y_me
     q_me = p_me * 2 + core
-    reducer = p_me < REDUCERS
-    idle = p_me >= REDUCERS
+    mine = pl.ds(p_me * ROWS_EACH, ROWS_EACH)
     lon_z = z_me * 2
 
     loads = []
@@ -185,8 +184,6 @@
     wi_f[LEVELS + 1 : LEVELS + 2, :] = bias_mid
     wi_f[LEVELS + 2 : LEVELS + 3, :] = bias_lo
     wi_b[...] = wi_f[...].astype(BF16)
-    for c in range(2):
-        wi_half[c] = wi_f[0:PAD, c * HALF : (c + 1) * HALF]
     w1t[...] = wi_f[...].T.astype(BF16)
     wo_f[LEVELS:LANES, :] = jnp.zeros((LANES - LEVELS, HIDDEN), F32)
     wo_f[0:LEVELS, :] = w_out_v[...].astype(F32)
@@ -354,33 +351,33 @@
     contract_last = (((1,), (1,)), ((), ()))
     sources = ((inp, dpre), (dlog, hid))
 
-    def half_of(m, c):
+    def half_into(ref, m, c):
         small, big = sources[m]
         rows = big[pl.ds(pl.multiple_of(c * HALF, HALF), HALF), :]
         value = lax.dot_general(small[...], rows, contract_last, preferred_element_type=F32)
-        return value[0:PAD].reshape(REDUCERS, 8, HALF)
-
-    for m in range(2):
-        given[m] = half_of(m, 1 - core)
+        ref[m, 0:PAD, :] = value[0:PAD, 0:LANES]
+        ref[m, PAD : 2 * PAD, :] = value[0:PAD, LANES:HALF]
+
+    for m in range(2):
+        half_into(given, m, 1 - core)
         post(given.at[m], from_core.at[m], partner, core_send.at[m], core_recv.at[m])
     for m in range(2):
-        kept[m] = half_of(m, core)
-    bout_row = lax.dot_general(
-        jnp.ones((16, COLS), BF16), dlog[...], contract_last, preferred_element_type=F32
-    )[0:1]
-    tile, first = LEVELS // 8, LEVELS % 8
+        half_into(kept, m, core)
 
     for m in range(2):
         drain(from_core.at[m], core_recv.at[m])
         half[m] = kept[m] + from_core[m]
         if m:
-            half[1, tile, first : first + 1, 0:LANES] = bout_row
+            half[1, LEVELS : LEVELS + 1, :] = lax.dot_general(
+                jnp.ones((16, COLS), BF16), dlog[...], contract_last, preferred_element_type=F32
+            )[0:1]
         for dx, dy in same_core:
             p, dev = chip_peer(dx, dy, 0)
-
-            @pl.when(p < REDUCERS)
-            def _(m=m, p=p, dev=dev):
-                post(half.at[m, p], from_plane.at[m, p_me], dev, plane_send.at[m], plane_recv.at[m])
+            post(
+                half.at[m, pl.ds(p * ROWS_EACH, ROWS_EACH)], from_plane.at[m, p_me], dev,
+                plane_send.at[m], plane_recv.at[m],
+            )
+        from_plane[m, p_me] = half[m, mine, :]
 
     hi = jnp.zeros((LEVELS, LANES), F32)
     lo = jnp.zeros((LEVELS, LANES), F32)
@@ -401,28 +398,21 @@
 
     scale = 1.0 / math.sqrt(count)
     for m in range(2):
-
-        @pl.when(reducer)
-        def _(m=m):
-            from_plane[m, p_me] = half[m, p_me]
-            drain(from_plane.at[m, pl.ds(0, CHIPS - 1)], plane_recv.at[m])
-            mid[m] = jnp.sum(from_plane[m], axis=0)
-            from_z[m, z_me] = mid[m]
-            send_z(mid.at[m], from_z.at[m], z_send.at[m], z_recv.at[m])
+        drain(from_plane.at[m, pl.ds(0, CHIPS - 1)], plane_recv.at[m])
+        mid[m] = jnp.sum(from_plane[m], axis=0)
+        from_z[m, z_me] = mid[m]
+        send_z(mid.at[m], from_z.at[m], z_send.at[m], z_recv.at[m])
 
     halo2_copies = send_halo(
         1, (adj_slabs.at[ROWS - 1], adj_slabs.at[0], edge2_hi, edge2_lo), halo2
     )
     for m in range(2):
-
-        @pl.when(reducer)
-        def _(m=m):
-            drain(from_z.at[m, pl.ds(0, DEPTH - 1)], z_recv.at[m])
-            chunk[m] = jnp.sum(from_z[m], axis=0) * scale
-            full[m, core, p_me] = chunk[m]
-            for dx, dy in same_core:
-                _, dev = chip_peer(dx, dy, 0)
-                post(chunk.at[m], full.at[m, core, p_me], dev, gather_send.at[m], gather_recv.at[m])
+        drain(from_z.at[m, pl.ds(0, DEPTH - 1)], z_recv.at[m])
+        chunk[m] = jnp.sum(from_z[m], axis=0) * scale
+        for dx, dy in same_core:
+            _, dev = chip_peer(dx, dy, 0)
+            post(chunk.at[m], full.at[m, core, mine], dev, gather_send.at[m], gather_recv.at[m])
+        full[m, core, mine, :] = chunk[m]
 
     for copy in halo2_copies:
         copy.wait_recv()
@@ -431,41 +421,33 @@
         wet = row_f < slabs[i, LEVELS : LEVELS + 1, :]
         din[i] = flux(centre, near, i) + jnp.where(wet, din[i], 0.0)
 
-    def drain_peers(ref, sem):
-        @pl.when(reducer)
-        def _():
-            drain(ref.at[pl.ds(0, REDUCERS - 1)], sem)
-
-        @pl.when(idle)
-        def _():
-            drain(ref, sem)
-
-    for m in range(2):
-        drain_peers(full.at[m, core], gather_recv.at[m])
+    peers_rows = pl.ds(0, (CHIPS - 1) * ROWS_EACH)
+    for m in range(2):
+        drain(full.at[m, core, peers_rows], gather_recv.at[m])
         post(full.at[m, core], full.at[m, core], partner, fwd_send.at[m], fwd_recv.at[m])
 
     def deliver(m, ref):
-        for p in range(REDUCERS):
-            rows = min(8, LEVELS - 8 * p)
-            for c in range(2):
-                ref[8 * p : 8 * p + rows, c * HALF : (c + 1) * HALF] = full[m, c, p, 0:rows, :]
+        for c in range(2):
+            for h in range(2):
+                n = 2 * c + h
+                ref[:, n * LANES : (n + 1) * LANES] = full[m, c, h * PAD : h * PAD + LEVELS, :]
 
     drain(full.at[0, 1 - core], fwd_recv.at[0])
-    weighted = jnp.zeros((PAD, HALF), F32)
+    weighted = jnp.zeros((PAD, LANES), F32)
     for c in range(2):
-        weighted = weighted + wi_half[c] * full[0, c].reshape(PAD, HALF)
+        for h in range(2):
+            n = 2 * c + h
+            part = full[0, c, h * PAD : (h + 1) * PAD, :]
+            weighted = weighted + wi_f[0:PAD, n * LANES : (n + 1) * LANES] * part
+            gb_in_ref[:, n * LANES : (n + 1) * LANES] = part[LEVELS : LEVELS + 1, :]
     level_sum = radius * jnp.sum(weighted, axis=1, keepdims=True) * math.sqrt(count)
     level_scale = level_sum / (count * radius * radius * radius)
     for i in range(ROWS):
         out_ref[:, i, :] = (din[i] - wet_slab(i) * level_scale)[0:LEVELS]
     deliver(0, gw_in_ref)
-    for c in range(2):
-        gb_in_ref[:, c * HALF : (c + 1) * HALF] = full[0, c, tile, first : first + 1, :]
     drain(full.at[1, 1 - core], fwd_recv.at[1])
     deliver(1, gw_out_ref)
-    gb_out_ref[...] = (
-        full[1, 0, tile, first : first + 1, 0:LANES] + full[1, 1, tile, first : first + 1, 0:LANES]
-    )
+    gb_out_ref[...] = full[1, 0, LEVELS : LEVELS + 1, :] + full[1, 1, LEVELS : LEVELS + 1, :]
 
     for copy in halo_copies + halo2_copies:
         copy.wait_send()
@@ -473,13 +455,9 @@
     drain(small_r2.at[pl.ds(0, DEPTH - 1)], small_send.at[1])
     for m in range(2):
         drain(from_core.at[m], core_send.at[m])
-        drain_peers(half.at[m], plane_send.at[m])
-
-        @pl.when(reducer)
-        def _(m=m):
-            drain(from_z.at[m, pl.ds(0, DEPTH - 1)], z_send.at[m])
-            drain(from_plane.at[m, pl.ds(0, CHIPS - 1)], gather_send.at[m])
-
+        drain(from_plane.at[m, pl.ds(0, CHIPS - 1)], plane_send.at[m])
+        drain(from_z.at[m, pl.ds(0, DEPTH - 1)], z_send.at[m])
+        drain(full.at[m, core, peers_rows], gather_send.at[m])
         drain(full.at[m, core], fwd_send.at[m])
 
 
@@ -501,7 +479,8 @@
     slab = (ROWS, PAD, LANES)
     levels = (LEVELS, ROWS, LANES)
     edge = (PAD, LANES)
-    pieces = (REDUCERS, 8, HALF)
+    flat = (2 * PAD, LANES)
+    piece = (ROWS_EACH, LANES)
 
     def v(*shape, dtype=F32):
         return pltpu.VMEM(shape, dtype)
@@ -516,14 +495,14 @@
         v(*slab), v(*slab), v(*edge), v(*edge), v(*edge), v(*edge),
         v(4, *edge), v(4, *edge), v(4 * ROWS, LANES),
         v(1, LANES), v(PLANE, 1, LANES), v(1, LANES), v(DEPTH, 1, LANES),
-        v(LANES, HIDDEN), v(2, PAD, HALF), v(LANES, HIDDEN), v(LANES, HIDDEN, dtype=BF16),
+        v(LANES, HIDDEN), v(LANES, HIDDEN), v(LANES, HIDDEN, dtype=BF16),
         v(HIDDEN, LANES, dtype=BF16), v(LANES, HIDDEN, dtype=BF16), v(HIDDEN, LANES, dtype=BF16),
         v(LANES, COLS, dtype=BF16), v(HIDDEN, COLS, dtype=BF16), v(HIDDEN, COLS),
         v(HIDDEN, COLS, dtype=BF16), v(LANES, COLS, dtype=BF16), v(*slab),
         v(*levels), v(*levels), v(*levels), v(*levels), v(LEVELS + 1, ROWS, LANES),
         v(*levels), v(*levels), v(*levels), v(LANES, ROWS, LANES),
-        v(2, *pieces), v(2, *pieces), v(2, *pieces), v(2, *pieces), v(2, CHIPS, 8, HALF),
-        v(2, 8, HALF), v(2, DEPTH, 8, HALF), v(2, 8, HALF), v(2, 2, *pieces),
+        v(2, *flat), v(2, *flat), v(2, *flat), v(2, *flat), v(2, CHIPS, *piece),
+        v(2, *piece), v(2, DEPTH, *piece), v(2, *piece), v(2, 2, *flat),
         sems(9), sems(2), sems(2), sems(2), sems(2), sems(2), sems(2),
         sems(2), sems(2), sems(2), sems(2), sems(2), sems(2), sems(8), sems(8),
     ]

time: 45.2 us -> 44.7 us (0.989)
  Pallas kernels: 44.5 us -> 44 us
    pallas_call x1, Pallas kernels: 43 us -> 42.5 us  [shards(): pl.pallas_call(kernel, out_shape=shapes, in_specs=[hbm] * 9, out_specs=(v...]
where the time goes in v6:
time: 44.7 us; the launch traced here: 44.6 us
  Pallas kernels  44 us (98%)
  between operations  0.64 us (1%)
    pallas_call x1, Pallas kernels, shards(): pl.pallas_call(kernel, out_shape=shapes, in_specs=[hbm] * 9, out_specs=(v...  42.5 us
    pallas_call x1, Pallas kernels, shards(): pl.pallas_call(store_results, out_shape=shapes[:2] + (jax.ShapeDtypeStruc...  1.5 us

profile of v6, /device:TPU:1, one launch (start us, length us, event | category | flops | bytes accessed | tf_op | source)
XLA Modules:
  0.0 44.6 jit_solution(8575881027958236572)
XLA Ops:
  0.6 42.5 %step_adjoint.1 = (f32[100,8,128]{2,1,0:T(8,128)S(1)}, f32[100,512]{1,0:T(8,128)S(1)}, f32[1,512]{1,0:T(1,128)S(1)}, f32[100,512]{1,0:T(8,128)S(1)}, f32[1,128]{1,0:T(1,128)S(1)}) custom-call(f32[100,8,128]{2,1,0:T(8,128)} %tracer_hbm.1, f32[100,8,128]{2,1,0:T(8,128)} %cot_hbm.1, s32[8,128]{1,0:T(8,128)} %land_hbm.1, s32[8,128]{1,0:T(8,128)} %bottom_hbm.1, ...), custom_call_target="tpu_custom_call" | custom-call | tf_op jit(solution)/shard_map/step_adjoint/pallas_call | solution.py:517
  43.1 1.5 %store_results.1 = (f32[100,8,128]{2,1,0:T(8,128)}, f32[100,512]{1,0:T(8,128)}, f32[512]{0:T(512)}, f32[100,512]{1,0:T(8,128)}, f32[100]{0:T(128)}) custom-call(f32[100,8,128]{2,1,0:T(8,128)S(1)} %get-tuple-element.15.out_v, f32[100,512]{1,0:T(8,128)S(1)} %get-tuple-element.16.gw_in_v, f32[1,512]{1,0:T(1,128)S(1)} %get-tuple-element.17.gb_in_v, ...), custom_call_target="tpu_custom_call" | custom-call | tf_op jit(solution)/shard_map/store_results/pallas_call | solution.py:528

commit v7 on v6

--- a/solution.py
+++ b/solution.py
@@ -51,7 +51,7 @@
     wi_f, wo_f, wi_b, w1t, wot, wo_b,
     inp, hid, slope, dpre, dlog, din,
     logit, mixed, val_x, val_y, mul_x, mul_y, gate, adj, dlev,
-    given, kept, from_core, half, from_plane, mid, from_z, chunk, full,
+    grad, from_core, half, from_plane, mid, from_z, chunk, full,
     load_sems, small_send, small_recv, core_send, core_recv, plane_send, plane_recv,
     z_send, z_recv, gather_send, gather_recv, fwd_send, fwd_recv, halo_send, halo_recv,
 ):
@@ -351,22 +351,17 @@
     contract_last = (((1,), (1,)), ((), ()))
     sources = ((inp, dpre), (dlog, hid))
 
-    def half_into(ref, m, c):
-        small, big = sources[m]
-        rows = big[pl.ds(pl.multiple_of(c * HALF, HALF), HALF), :]
-        value = lax.dot_general(small[...], rows, contract_last, preferred_element_type=F32)
-        ref[m, 0:PAD, :] = value[0:PAD, 0:LANES]
-        ref[m, PAD : 2 * PAD, :] = value[0:PAD, LANES:HALF]
-
-    for m in range(2):
-        half_into(given, m, 1 - core)
-        post(given.at[m], from_core.at[m], partner, core_send.at[m], core_recv.at[m])
-    for m in range(2):
-        half_into(kept, m, core)
+    for m, (small, big) in enumerate(sources):
+        value = lax.dot_general(small[...], big[...], contract_last, preferred_element_type=F32)
+        for n in range(4):
+            grad[m, n // 2, (n % 2) * PAD : (n % 2 + 1) * PAD, :] = value[
+                0:PAD, n * LANES : (n + 1) * LANES
+            ]
+        post(grad.at[m, 1 - core], from_core.at[m], partner, core_send.at[m], core_recv.at[m])
 
     for m in range(2):
         drain(from_core.at[m], core_recv.at[m])
-        half[m] = kept[m] + from_core[m]
+        half[m] = grad[m, core] + from_core[m]
         if m:
             half[1, LEVELS : LEVELS + 1, :] = lax.dot_general(
                 jnp.ones((16, COLS), BF16), dlog[...], contract_last, preferred_element_type=F32
@@ -461,14 +456,21 @@
         drain(full.at[m, core], fwd_send.at[m])
 
 
-def store_results(out_v, gw_in_v, gb_in_v, gw_out_v, gb_out_v, out_h, gw_in_h, gb_in_ref, gw_out_h, gb_out_ref, sems):
-    copies = []
-    for n, (src, dst) in enumerate(((out_v, out_h), (gw_in_v, gw_in_h), (gw_out_v, gw_out_h))):
-        copy = pltpu.make_async_copy(src, dst, sems.at[n])
+def store_results(
+    out_v, gw_in_v, gb_in_v, gw_out_v, gb_out_v, out_h, gw_in_h, gb_in_h, gw_out_h, gb_out_h,
+    gb_in_flat, gb_out_flat, sems,
+):
+    pairs = (
+        (out_v, out_h), (gw_in_v, gw_in_h), (gw_out_v, gw_out_h),
+        (gb_in_flat, gb_in_h), (gb_out_flat, gb_out_h),
+    )
+    copies = [pltpu.make_async_copy(src, dst, sems.at[n]) for n, (src, dst) in enumerate(pairs)]
+    for copy in copies[:3]:
         copy.start()
-        copies.append(copy)
-    gb_in_ref[...] = gb_in_v[...].reshape(HIDDEN)
-    gb_out_ref[...] = gb_out_v[...].reshape(LANES)[0:LEVELS]
+    gb_in_flat[...] = gb_in_v[...].reshape(HIDDEN)
+    gb_out_flat[...] = gb_out_v[...].reshape(LANES)[0:LEVELS]
+    for copy in copies[3:]:
+        copy.start()
     for copy in copies:
         copy.wait()
 
@@ -501,7 +503,7 @@
         v(HIDDEN, COLS, dtype=BF16), v(LANES, COLS, dtype=BF16), v(*slab),
         v(*levels), v(*levels), v(*levels), v(*levels), v(LEVELS + 1, ROWS, LANES),
         v(*levels), v(*levels), v(*levels), v(LANES, ROWS, LANES),
-        v(2, *flat), v(2, *flat), v(2, *flat), v(2, *flat), v(2, CHIPS, *piece),
+        v(2, 2, *flat), v(2, *flat), v(2, *flat), v(2, CHIPS, *piece),
         v(2, *piece), v(2, DEPTH, *piece), v(2, *piece), v(2, 2, *flat),
         sems(9), sems(2), sems(2), sems(2), sems(2), sems(2), sems(2),
         sems(2), sems(2), sems(2), sems(2), sems(2), sems(2), sems(8), sems(8),
@@ -530,8 +532,8 @@
         out_shape=shapes[:2]
         + (jax.ShapeDtypeStruct((HIDDEN,), F32), shapes[3], jax.ShapeDtypeStruct((LEVELS,), F32)),
         in_specs=[vmem] * 5,
-        out_specs=(hbm, hbm, vmem, hbm, vmem),
-        scratch_shapes=[sems(3)],
+        out_specs=(hbm,) * 5,
+        scratch_shapes=[v(HIDDEN), v(LEVELS), sems(5)],
         compiler_params=pltpu.CompilerParams(vmem_limit_bytes=1024 * 1024),
         name="store_results",
     )(*results)

time: 44.7 us -> 43.7 us (0.978)
  Pallas kernels: 44 us -> 43 us
    pallas_call x1, Pallas kernels: 1.5 us -> 0.94 us  [shards(): pl.pallas_call(store_results, out_shape=shapes[:2] + (jax.ShapeDtypeStruc...]
where the time goes in v7:
time: 43.7 us; the launch traced here: 43.6 us
  Pallas kernels  43 us (98%)
  between operations  0.64 us (1%)
    pallas_call x1, Pallas kernels, shards(): pl.pallas_call(kernel, out_shape=shapes, in_specs=[hbm] * 9, out_specs=(v...  42 us
    pallas_call x1, Pallas kernels, shards(): pl.pallas_call(store_results, out_shape=shapes[:2] + (jax.ShapeDtypeStruc...  0.94 us

profile of v7, /device:TPU:1, one launch (start us, length us, event | category | flops | bytes accessed | tf_op | source)
XLA Modules:
  0.0 43.6 jit_solution(7673387909366342070)
XLA Ops:
  0.6 42.0 %step_adjoint.1 = (f32[100,8,128]{2,1,0:T(8,128)S(1)}, f32[100,512]{1,0:T(8,128)S(1)}, f32[1,512]{1,0:T(1,128)S(1)}, f32[100,512]{1,0:T(8,128)S(1)}, f32[1,128]{1,0:T(1,128)S(1)}) custom-call(f32[100,8,128]{2,1,0:T(8,128)} %tracer_hbm.1, f32[100,8,128]{2,1,0:T(8,128)} %cot_hbm.1, s32[8,128]{1,0:T(8,128)} %land_hbm.1, s32[8,128]{1,0:T(8,128)} %bottom_hbm.1, ...), custom_call_target="tpu_custom_call" | custom-call | tf_op jit(solution)/shard_map/step_adjoint/pallas_call | solution.py:519
  42.7 0.9 %store_results.1 = (f32[100,8,128]{2,1,0:T(8,128)}, f32[100,512]{1,0:T(8,128)}, f32[512]{0:T(512)}, f32[100,512]{1,0:T(8,128)}, f32[100]{0:T(128)}) custom-call(f32[100,8,128]{2,1,0:T(8,128)S(1)} %get-tuple-element.15.out_v, f32[100,512]{1,0:T(8,128)S(1)} %get-tuple-element.16.gw_in_v, f32[1,512]{1,0:T(1,128)S(1)} %get-tuple-element.17.gb_in_v, ...), custom_call_target="tpu_custom_call" | custom-call | tf_op jit(solution)/shard_map/store_results/pallas_call | solution.py:530

commit v8 on v7

--- a/solution.py
+++ b/solution.py
@@ -53,7 +53,7 @@
     logit, mixed, val_x, val_y, mul_x, mul_y, gate, adj, dlev,
     grad, from_core, half, from_plane, mid, from_z, chunk, full,
     load_sems, small_send, small_recv, core_send, core_recv, plane_send, plane_recv,
-    z_send, z_recv, gather_send, gather_recv, fwd_send, fwd_recv, halo_send, halo_recv,
+    z_send, z_recv, gather_send, gather_recv, far_recv, fwd_send, fwd_recv, halo_send, halo_recv,
 ):
     lat = lax.axis_index("lat")
     lon = lax.axis_index("lon")
@@ -91,6 +91,8 @@
 
     everyone = [(dx, dy, dc) for dx, dy in CHIP_STEPS for dc in (0, 1) if dx or dy or dc]
     same_core = [(dx, dy) for dx, dy in CHIP_STEPS if dx or dy]
+    far_steps = [s for s in same_core if ring(s[0], SIDE) + ring(s[1], SIDE) > 2]
+    near_steps = [s for s in same_core if s not in far_steps]
     partner = (lat, lon + 1 - 2 * core)
 
     barrier = pltpu.get_barrier_semaphore()
@@ -404,9 +406,13 @@
     for m in range(2):
         drain(from_z.at[m, pl.ds(0, DEPTH - 1)], z_recv.at[m])
         chunk[m] = jnp.sum(from_z[m], axis=0) * scale
-        for dx, dy in same_core:
-            _, dev = chip_peer(dx, dy, 0)
-            post(chunk.at[m], full.at[m, core, mine], dev, gather_send.at[m], gather_recv.at[m])
+        place = full.at[m, core, mine]
+        for dx, dy in far_steps:
+            post(chunk.at[m], place, chip_peer(dx, dy, 0)[1], gather_send.at[m], far_recv.at[m])
+            post(chunk.at[m], place, chip_peer(dx, dy, 1)[1], fwd_send.at[m], fwd_recv.at[m])
+        for dx, dy in near_steps:
+            post(chunk.at[m], place, chip_peer(dx, dy, 0)[1], gather_send.at[m], gather_recv.at[m])
+        post(chunk.at[m], place, partner, fwd_send.at[m], fwd_recv.at[m])
         full[m, core, mine, :] = chunk[m]
 
     for copy in halo2_copies:
@@ -418,8 +424,14 @@
 
     peers_rows = pl.ds(0, (CHIPS - 1) * ROWS_EACH)
     for m in range(2):
-        drain(full.at[m, core, peers_rows], gather_recv.at[m])
-        post(full.at[m, core], full.at[m, core], partner, fwd_send.at[m], fwd_recv.at[m])
+        drain(full.at[m, core, pl.ds(0, len(near_steps) * ROWS_EACH)], gather_recv.at[m])
+        for dx, dy in near_steps:
+            place = full.at[m, core, pl.ds(chip_peer(dx, dy, 0)[0] * ROWS_EACH, ROWS_EACH)]
+            post(place, place, partner, fwd_send.at[m], fwd_recv.at[m])
+
+    def await_all(m):
+        drain(full.at[m, core, pl.ds(0, len(far_steps) * ROWS_EACH)], far_recv.at[m])
+        drain(full.at[m, 1 - core], fwd_recv.at[m])
 
     def deliver(m, ref):
         for c in range(2):
@@ -427,7 +439,7 @@
                 n = 2 * c + h
                 ref[:, n * LANES : (n + 1) * LANES] = full[m, c, h * PAD : h * PAD + LEVELS, :]
 
-    drain(full.at[0, 1 - core], fwd_recv.at[0])
+    await_all(0)
     weighted = jnp.zeros((PAD, LANES), F32)
     for c in range(2):
         for h in range(2):
@@ -440,7 +452,7 @@
     for i in range(ROWS):
         out_ref[:, i, :] = (din[i] - wet_slab(i) * level_scale)[0:LEVELS]
     deliver(0, gw_in_ref)
-    drain(full.at[1, 1 - core], fwd_recv.at[1])
+    await_all(1)
     deliver(1, gw_out_ref)
     gb_out_ref[...] = full[1, 0, LEVELS : LEVELS + 1, :] + full[1, 1, LEVELS : LEVELS + 1, :]
 
@@ -506,7 +518,7 @@
         v(2, 2, *flat), v(2, *flat), v(2, *flat), v(2, CHIPS, *piece),
         v(2, *piece), v(2, DEPTH, *piece), v(2, *piece), v(2, 2, *flat),
         sems(9), sems(2), sems(2), sems(2), sems(2), sems(2), sems(2),
-        sems(2), sems(2), sems(2), sems(2), sems(2), sems(2), sems(8), sems(8),
+        sems(2), sems(2), sems(2), sems(2), sems(2), sems(2), sems(2), sems(8), sems(8),
     ]
     shapes = (
         jax.ShapeDtypeStruct(tracer.shape, F32),

time: 43.7 us -> 44.4 us (1.016)
  Pallas kernels: 43 us -> 43.6 us
    pallas_call x1, Pallas kernels: 42 us -> 42.7 us  [shards(): pl.pallas_call(kernel, out_shape=shapes, in_specs=[hbm] * 9, out_specs=(v...]
where the time goes in v8:
time: 44.4 us; the launch traced here: 44.3 us
  Pallas kernels  43.6 us (98%)
  between operations  0.64 us (1%)
    pallas_call x1, Pallas kernels, shards(): pl.pallas_call(kernel, out_shape=shapes, in_specs=[hbm] * 9, out_specs=(v...  42.7 us
    pallas_call x1, Pallas kernels, shards(): pl.pallas_call(store_results, out_shape=shapes[:2] + (jax.ShapeDtypeStruc...  0.94 us

profile of v8, /device:TPU:1, one launch (start us, length us, event | category | flops | bytes accessed | tf_op | source)
XLA Modules:
  0.0 44.3 jit_solution(2076098799810045818)
XLA Ops:
  0.6 42.7 %step_adjoint.1 = (f32[100,8,128]{2,1,0:T(8,128)S(1)}, f32[100,512]{1,0:T(8,128)S(1)}, f32[1,512]{1,0:T(1,128)S(1)}, f32[100,512]{1,0:T(8,128)S(1)}, f32[1,128]{1,0:T(1,128)S(1)}) custom-call(f32[100,8,128]{2,1,0:T(8,128)} %tracer_hbm.1, f32[100,8,128]{2,1,0:T(8,128)} %cot_hbm.1, s32[8,128]{1,0:T(8,128)} %land_hbm.1, s32[8,128]{1,0:T(8,128)} %bottom_hbm.1, ...), custom_call_target="tpu_custom_call" | custom-call | tf_op jit(solution)/shard_map/step_adjoint/pallas_call | solution.py:531
  43.3 0.9 %store_results.1 = (f32[100,8,128]{2,1,0:T(8,128)}, f32[100,512]{1,0:T(8,128)}, f32[512]{0:T(512)}, f32[100,512]{1,0:T(8,128)}, f32[100]{0:T(128)}) custom-call(f32[100,8,128]{2,1,0:T(8,128)S(1)} %get-tuple-element.15.out_v, f32[100,512]{1,0:T(8,128)S(1)} %get-tuple-element.16.gw_in_v, f32[1,512]{1,0:T(1,128)S(1)} %get-tuple-element.17.gb_in_v, ...), custom_call_target="tpu_custom_call" | custom-call | tf_op jit(solution)/shard_map/store_results/pallas_call | solution.py:542

commit v9 on v7

--- a/solution.py
+++ b/solution.py
@@ -366,13 +366,14 @@
             half[1, LEVELS : LEVELS + 1, :] = lax.dot_general(
                 jnp.ones((16, COLS), BF16), dlog[...], contract_last, preferred_element_type=F32
             )[0:1]
-        for dx, dy in same_core:
-            p, dev = chip_peer(dx, dy, 0)
-            post(
-                half.at[m, pl.ds(p * ROWS_EACH, ROWS_EACH)], from_plane.at[m, p_me], dev,
-                plane_send.at[m], plane_recv.at[m],
-            )
-        from_plane[m, p_me] = half[m, mine, :]
+    for dx, dy in same_core:
+        p, dev = chip_peer(dx, dy, 0)
+        post(
+            half.at[:, pl.ds(p * ROWS_EACH, ROWS_EACH)], from_plane.at[p_me], dev,
+            plane_send.at[0], plane_recv.at[0],
+        )
+    for m in range(2):
+        from_plane[p_me, m] = half[m, mine, :]
 
     hi = jnp.zeros((LEVELS, LANES), F32)
     lo = jnp.zeros((LEVELS, LANES), F32)
@@ -392,22 +393,21 @@
             din[i] = out[0:PAD, s * LANES : (s + 1) * LANES] * inv_radius
 
     scale = 1.0 / math.sqrt(count)
-    for m in range(2):
-        drain(from_plane.at[m, pl.ds(0, CHIPS - 1)], plane_recv.at[m])
-        mid[m] = jnp.sum(from_plane[m], axis=0)
-        from_z[m, z_me] = mid[m]
-        send_z(mid.at[m], from_z.at[m], z_send.at[m], z_recv.at[m])
+    drain(from_plane.at[pl.ds(0, CHIPS - 1)], plane_recv.at[0])
+    mid[...] = jnp.sum(from_plane[...], axis=0)
+    from_z[z_me] = mid[...]
+    send_z(mid, from_z, z_send.at[0], z_recv.at[0])
 
     halo2_copies = send_halo(
         1, (adj_slabs.at[ROWS - 1], adj_slabs.at[0], edge2_hi, edge2_lo), halo2
     )
+    drain(from_z.at[pl.ds(0, DEPTH - 1)], z_recv.at[0])
+    chunk[...] = jnp.sum(from_z[...], axis=0) * scale
+    for dx, dy in same_core:
+        _, dev = chip_peer(dx, dy, 0)
+        post(chunk, full.at[core, :, mine], dev, gather_send.at[0], gather_recv.at[0])
     for m in range(2):
-        drain(from_z.at[m, pl.ds(0, DEPTH - 1)], z_recv.at[m])
-        chunk[m] = jnp.sum(from_z[m], axis=0) * scale
-        for dx, dy in same_core:
-            _, dev = chip_peer(dx, dy, 0)
-            post(chunk.at[m], full.at[m, core, mine], dev, gather_send.at[m], gather_recv.at[m])
-        full[m, core, mine, :] = chunk[m]
+        full[core, m, mine, :] = chunk[m]
 
     for copy in halo2_copies:
         copy.wait_recv()
@@ -417,22 +417,22 @@
         din[i] = flux(centre, near, i) + jnp.where(wet, din[i], 0.0)
 
     peers_rows = pl.ds(0, (CHIPS - 1) * ROWS_EACH)
+    drain(full.at[core, :, peers_rows], gather_recv.at[0])
     for m in range(2):
-        drain(full.at[m, core, peers_rows], gather_recv.at[m])
-        post(full.at[m, core], full.at[m, core], partner, fwd_send.at[m], fwd_recv.at[m])
+        post(full.at[core, m], full.at[core, m], partner, fwd_send.at[m], fwd_recv.at[m])
 
     def deliver(m, ref):
         for c in range(2):
             for h in range(2):
                 n = 2 * c + h
-                ref[:, n * LANES : (n + 1) * LANES] = full[m, c, h * PAD : h * PAD + LEVELS, :]
-
-    drain(full.at[0, 1 - core], fwd_recv.at[0])
+                ref[:, n * LANES : (n + 1) * LANES] = full[c, m, h * PAD : h * PAD + LEVELS, :]
+
+    drain(full.at[1 - core, 0], fwd_recv.at[0])
     weighted = jnp.zeros((PAD, LANES), F32)
     for c in range(2):
         for h in range(2):
             n = 2 * c + h
-            part = full[0, c, h * PAD : (h + 1) * PAD, :]
+            part = full[c, 0, h * PAD : (h + 1) * PAD, :]
             weighted = weighted + wi_f[0:PAD, n * LANES : (n + 1) * LANES] * part
             gb_in_ref[:, n * LANES : (n + 1) * LANES] = part[LEVELS : LEVELS + 1, :]
     level_sum = radius * jnp.sum(weighted, axis=1, keepdims=True) * math.sqrt(count)
@@ -440,20 +440,20 @@
     for i in range(ROWS):
         out_ref[:, i, :] = (din[i] - wet_slab(i) * level_scale)[0:LEVELS]
     deliver(0, gw_in_ref)
-    drain(full.at[1, 1 - core], fwd_recv.at[1])
+    drain(full.at[1 - core, 1], fwd_recv.at[1])
     deliver(1, gw_out_ref)
-    gb_out_ref[...] = full[1, 0, LEVELS : LEVELS + 1, :] + full[1, 1, LEVELS : LEVELS + 1, :]
+    gb_out_ref[...] = full[0, 1, LEVELS : LEVELS + 1, :] + full[1, 1, LEVELS : LEVELS + 1, :]
 
     for copy in halo_copies + halo2_copies:
         copy.wait_send()
     drain(small_r1.at[pl.ds(0, PLANE - 1)], small_send.at[0])
     drain(small_r2.at[pl.ds(0, DEPTH - 1)], small_send.at[1])
+    drain(from_plane.at[pl.ds(0, CHIPS - 1)], plane_send.at[0])
+    drain(from_z.at[pl.ds(0, DEPTH - 1)], z_send.at[0])
+    drain(full.at[core, :, peers_rows], gather_send.at[0])
     for m in range(2):
         drain(from_core.at[m], core_send.at[m])
-        drain(from_plane.at[m, pl.ds(0, CHIPS - 1)], plane_send.at[m])
-        drain(from_z.at[m, pl.ds(0, DEPTH - 1)], z_send.at[m])
-        drain(full.at[m, core, peers_rows], gather_send.at[m])
-        drain(full.at[m, core], fwd_send.at[m])
+        drain(full.at[core, m], fwd_send.at[m])
 
 
 def store_results(
@@ -503,10 +503,10 @@
         v(HIDDEN, COLS, dtype=BF16), v(LANES, COLS, dtype=BF16), v(*slab),
         v(*levels), v(*levels), v(*levels), v(*levels), v(LEVELS + 1, ROWS, LANES),
         v(*levels), v(*levels), v(*levels), v(LANES, ROWS, LANES),
-        v(2, 2, *flat), v(2, *flat), v(2, *flat), v(2, CHIPS, *piece),
-        v(2, *piece), v(2, DEPTH, *piece), v(2, *piece), v(2, 2, *flat),
-        sems(9), sems(2), sems(2), sems(2), sems(2), sems(2), sems(2),
-        sems(2), sems(2), sems(2), sems(2), sems(2), sems(2), sems(8), sems(8),
+        v(2, 2, *flat), v(2, *flat), v(2, *flat), v(CHIPS, 2, *piece),
+        v(2, *piece), v(DEPTH, 2, *piece), v(2, *piece), v(2, 2, *flat),
+        sems(9), sems(2), sems(2), sems(2), sems(2), sems(1), sems(1),
+        sems(1), sems(1), sems(1), sems(1), sems(2), sems(2), sems(8), sems(8),
     ]
     shapes = (
         jax.ShapeDtypeStruct(tracer.shape, F32),

time: 43.7 us -> 44.8 us (1.025)
  Pallas kernels: 43 us -> 44 us
    pallas_call x1, Pallas kernels: 42 us -> 43.1 us  [shards(): pl.pallas_call(kernel, out_shape=shapes, in_specs=[hbm] * 9, out_specs=(v...]
where the time goes in v9:
time: 44.8 us; the launch traced here: 44.7 us
  Pallas kernels  44 us (98%)
  between operations  0.64 us (1%)
    pallas_call x1, Pallas kernels, shards(): pl.pallas_call(kernel, out_shape=shapes, in_specs=[hbm] * 9, out_specs=(v...  43.1 us
    pallas_call x1, Pallas kernels, shards(): pl.pallas_call(store_results, out_shape=shapes[:2] + (jax.ShapeDtypeStruc...  0.94 us

profile of v9, /device:TPU:1, one launch (start us, length us, event | category | flops | bytes accessed | tf_op | source)
XLA Modules:
  0.0 44.7 jit_solution(3679135461138403899)
XLA Ops:
  0.6 43.1 %step_adjoint.1 = (f32[100,8,128]{2,1,0:T(8,128)S(1)}, f32[100,512]{1,0:T(8,128)S(1)}, f32[1,512]{1,0:T(1,128)S(1)}, f32[100,512]{1,0:T(8,128)S(1)}, f32[1,128]{1,0:T(1,128)S(1)}) custom-call(f32[100,8,128]{2,1,0:T(8,128)} %tracer_hbm.1, f32[100,8,128]{2,1,0:T(8,128)} %cot_hbm.1, s32[8,128]{1,0:T(8,128)} %land_hbm.1, s32[8,128]{1,0:T(8,128)} %bottom_hbm.1, ...), custom_call_target="tpu_custom_call" | custom-call | tf_op jit(solution)/shard_map/step_adjoint/pallas_call | solution.py:519
  43.7 0.9 %store_results.1 = (f32[100,8,128]{2,1,0:T(8,128)}, f32[100,512]{1,0:T(8,128)}, f32[512]{0:T(512)}, f32[100,512]{1,0:T(8,128)}, f32[100]{0:T(128)}) custom-call(f32[100,8,128]{2,1,0:T(8,128)S(1)} %get-tuple-element.15.out_v, f32[100,512]{1,0:T(8,128)S(1)} %get-tuple-element.16.gw_in_v, f32[1,512]{1,0:T(1,128)S(1)} %get-tuple-element.17.gb_in_v, ...), custom_call_target="tpu_custom_call" | custom-call | tf_op jit(solution)/shard_map/store_results/pallas_call | solution.py:530

commit v10 on v7

--- a/solution.py
+++ b/solution.py
@@ -359,13 +359,15 @@
             ]
         post(grad.at[m, 1 - core], from_core.at[m], partner, core_send.at[m], core_recv.at[m])
 
+    bout_row = lax.dot_general(
+        jnp.ones((16, COLS), BF16), dlog[...], contract_last, preferred_element_type=F32
+    )[0:1]
+
     for m in range(2):
         drain(from_core.at[m], core_recv.at[m])
         half[m] = grad[m, core] + from_core[m]
         if m:
-            half[1, LEVELS : LEVELS + 1, :] = lax.dot_general(
-                jnp.ones((16, COLS), BF16), dlog[...], contract_last, preferred_element_type=F32
-            )[0:1]
+            half[1, LEVELS : LEVELS + 1, :] = bout_row
         for dx, dy in same_core:
             p, dev = chip_peer(dx, dy, 0)
             post(

time: 43.7 us -> 43.9 us (level)
  no operation moved by 1% of the time
where the time goes in v10:
time: 43.9 us; the launch traced here: 43.8 us
  Pallas kernels  43.1 us (98%)
  between operations  0.64 us (1%)
    pallas_call x1, Pallas kernels, shards(): pl.pallas_call(kernel, out_shape=shapes, in_specs=[hbm] * 9, out_specs=(v...  42.2 us
    pallas_call x1, Pallas kernels, shards(): pl.pallas_call(store_results, out_shape=shapes[:2] + (jax.ShapeDtypeStruc...  0.94 us

profile of v10, /device:TPU:1, one launch (start us, length us, event | category | flops | bytes accessed | tf_op | source)
XLA Modules:
  0.0 43.8 jit_solution(14570446447910925098)
XLA Ops:
  0.6 42.2 %step_adjoint.1 = (f32[100,8,128]{2,1,0:T(8,128)S(1)}, f32[100,512]{1,0:T(8,128)S(1)}, f32[1,512]{1,0:T(1,128)S(1)}, f32[100,512]{1,0:T(8,128)S(1)}, f32[1,128]{1,0:T(1,128)S(1)}) custom-call(f32[100,8,128]{2,1,0:T(8,128)} %tracer_hbm.1, f32[100,8,128]{2,1,0:T(8,128)} %cot_hbm.1, s32[8,128]{1,0:T(8,128)} %land_hbm.1, s32[8,128]{1,0:T(8,128)} %bottom_hbm.1, ...), custom_call_target="tpu_custom_call" | custom-call | tf_op jit(solution)/shard_map/step_adjoint/pallas_call | solution.py:521
  42.8 0.9 %store_results.1 = (f32[100,8,128]{2,1,0:T(8,128)}, f32[100,512]{1,0:T(8,128)}, f32[512]{0:T(512)}, f32[100,512]{1,0:T(8,128)}, f32[100]{0:T(128)}) custom-call(f32[100,8,128]{2,1,0:T(8,128)S(1)} %get-tuple-element.15.out_v, f32[100,512]{1,0:T(8,128)S(1)} %get-tuple-element.16.gw_in_v, f32[1,512]{1,0:T(1,128)S(1)} %get-tuple-element.17.gb_in_v, ...), custom_call_target="tpu_custom_call" | custom-call | tf_op jit(solution)/shard_map/store_results/pallas_call | solution.py:532
